TPU v7x, 32 devices: a whole 2x2x4 slice. The times are simulated.
32 devices in a mesh: seq: 8 (over z, x), dp: 4 (over y, core).
Axes of the slice: x: 2, y: 2, z: 4, core: 2. Of those that a mesh axis runs over, the one named last changes fastest.
Arguments:
- layer_input: bfloat16 [4, 1024, 4096], P('dp', 'seq'), may hold values from -6 to 6
- projection: bfloat16 [4096, 256], replicated, may hold values from -0.09375 to 0.09375
- ssm_input: bfloat16 [4, 1024, 4096], P('dp', 'seq'), may hold values from -6 to 6
- step_logit: float32 [4, 1024, 64], P('dp', 'seq'), may hold values from -4 to 4
- decay_rate: float32 [64], replicated, may hold values from 0.00048828125 to 0.1
- output_grad: bfloat16 [4, 1024, 4096], P('dp', 'seq'), may hold values from -6 to 6
Outputs:
- input_grad: bfloat16 [4, 1024, 4096], P('dp', 'seq')
- step_grad: float32 [4, 1024, 64], P('dp', 'seq')
- rate_grad: float32 [64], replicated
- projection_grad: float32 [4096, 256], P('seq')
All inputs are finite; a program needn't handle non-finite values.
Results may differ from a plain program's by a relative error of at most 0.011.
Values sent between devices are 32-bit elements; how exact they have to be, the bound alone decides.
A program may use at most 320 MiB of HBM per device.

v0:
```python
import functools

import jax
import jax.numpy as jnp
from jax import lax
from jax.experimental import pallas as pl
from jax.experimental.pallas import tpu as pltpu
from jax.sharding import PartitionSpec as P

F32 = jnp.float32
BF16 = jnp.bfloat16
HEADS = 4


def dot(a, b, ca, cb):
    return lax.dot_general(a, b, (((ca,), (cb,)), ((), ())), preferred_element_type=F32)


def pair_columns(cols, j, size):
    rows = cols.shape[0]
    lane = lax.broadcasted_iota(jnp.int32, (rows, 2 * size), 1)
    return jnp.where(lane < size, cols[:, j : j + 1], cols[:, j + 1 : j + 2])


def layer_kernel(
    n, size, b_ref, c_ref, x_ref, g_ref, col_ref, row_ref, d_ref,
    dx_ref, rows_ref, cols_ref, ef_ref, gbc_ref,
    s_ref, a_ref, e_out, f_out, scores, d_scores, d_b, d_c,
    d_in, s_in, a_in, e_in, f_in, e_snd, f_snd,
    d_sem, s_sem, a_sem, e_sem, f_sem,
):
    chunks = s_ref.shape[0]
    length = b_ref.shape[0]
    state = b_ref.shape[1]
    width = 2 * size
    heads = chunks * HEADS
    nz = n // 2
    me = lax.axis_index("seq")
    odd = lax.rem(me, 2)
    z = lax.div(me, 2)
    partner = me + 1 - 2 * odd
    first, last = z == 0, z == nz - 1
    barrier = pltpu.get_barrier_semaphore()

    def greet(who):
        pl.semaphore_signal(
            barrier, inc=1, device_id={"seq": who}, device_id_type=pl.DeviceIdType.MESH
        )

    greet(partner)
    pl.when(jnp.logical_not(first))(lambda: greet(me - 2))
    pl.when(jnp.logical_not(last))(lambda: greet(me + 2))

    def send(src, dst, sems, k, who):
        return pltpu.make_async_remote_copy(
            src_ref=src, dst_ref=dst, send_sem=sems.at[0, k], recv_sem=sems.at[1, k],
            device_id={"seq": who}, device_id_type=pl.DeviceIdType.MESH,
        )

    def copy_d():
        return send(d_ref, d_in, d_sem, 0, partner)

    def copy_s(k):
        return send(s_ref.at[k], s_in.at[k], s_sem, k, partner)

    def copy_a(k):
        return send(a_ref.at[k], a_in.at[k], a_sem, k, partner)

    def copy_e(k):
        return send(e_snd.at[k], e_in.at[k], e_sem, k, me + 2)

    def copy_f(k):
        return send(f_snd.at[k], f_in.at[k], f_sem, k, me - 2)

    def pair_lanes(k, pair):
        return pl.ds(pl.multiple_of(k * (HEADS * size) + pair * width, width), width)

    def local(k, unused):
        cols = col_ref[k]
        for pair in range(HEADS // 2):
            lanes = pl.ds(pair * width, width)
            wide = pair_lanes(k, pair)
            j = 2 * pair
            to_end = pair_columns(cols, j + HEADS, size) * pair_columns(cols, j + 2 * HEADS, size)
            grow = pair_columns(cols, j + 3 * HEADS, size)
            xs = (x_ref[:, wide].astype(F32) * to_end).astype(BF16)
            gs = (g_ref[:, wide].astype(F32) * grow).astype(BF16)
            s_ref[k, :, lanes] = dot(b_ref[...], xs, 0, 0)
            a_ref[k, :, lanes] = dot(c_ref[...], gs, 0, 0)

        @pl.when(k > 0)
        def _():
            copy_s(k - 1).start()
            copy_a(k - 1).start()

        return unused

    end = jnp.logical_or(first, last)
    pl.when(end)(lambda: pl.semaphore_wait(barrier, min(nz, 2)))
    pl.when(jnp.logical_not(end))(lambda: pl.semaphore_wait(barrier, 3))
    copy_d().start()
    lax.fori_loop(0, chunks, local, 0)
    copy_s(chunks - 1).start()
    copy_a(chunks - 1).start()

    @pl.when(first)
    def _():
        e_in[...] = jnp.zeros_like(e_in)

    @pl.when(last)
    def _():
        f_in[...] = jnp.zeros_like(f_in)

    b, c = b_ref[...], c_ref[...]
    scores[...] = dot(b, c, 1, 1)
    d_scores[...] = jnp.zeros_like(d_scores)
    d_b[...] = jnp.zeros_like(d_b)
    d_c[...] = jnp.zeros_like(d_c)
    cols_ref[...] = jnp.zeros_like(cols_ref)
    copy_d().wait_recv()

    def advance(k, near, far, carry, out, snd, near_first):
        @pl.when(near_first)
        def _():
            value = carry[k]
            out[k] = value.astype(out.dtype)
            middle = d_ref[k, 0:1] * value + near[k]
            snd[k] = d_in[k, 0:1] * middle + far[k]

        @pl.when(jnp.logical_not(near_first))
        def _():
            middle = d_in[k, 0:1] * carry[k] + far[k]
            out[k] = middle.astype(out.dtype)
            snd[k] = d_ref[k, 0:1] * middle + near[k]

    def gradients(k):
        cols = col_ref[k]
        rows = row_ref[k]
        k_st = scores[...]
        causal = lax.broadcasted_iota(jnp.int32, (length, length), 1) >= lax.broadcasted_iota(
            jnp.int32, (length, length), 0
        )
        low = lax.broadcasted_iota(jnp.int32, (length, width), 1) < size
        place = lax.broadcasted_iota(jnp.int32, cols_ref.shape, 1) - k * HEADS
        result = cols_ref[...]
        q_sum = d_scores[...]
        b_sum, c_sum = d_b[...], d_c[...]
        for pair in range(HEADS // 2):
            lanes = pl.ds(pair * width, width)
            wide = pair_lanes(k, pair)
            x2, g2 = x_ref[:, wide], g_ref[:, wide]
            x2f, g2f = x2.astype(F32), g2.astype(F32)
            e2, f2 = e_out[k, :, lanes], f_out[k, :, lanes]
            j = 2 * pair
            dt2 = pair_columns(cols, j + HEADS, size)
            end2 = pair_columns(cols, j + 2 * HEADS, size)
            grow2 = pair_columns(cols, j + 3 * HEADS, size)
            g_low = jnp.where(low, g2, jnp.zeros_like(g2))
            g_high = jnp.where(low, jnp.zeros_like(g2), g2)
            g_both = jnp.concatenate([g_low, g_high], axis=0)
            gram = dot(x2, g_both, 1, 1)
            weights = []
            for side in range(2):
                h = j + side
                gap = rows[h : h + 1, :] - cols[:, h : h + 1]
                decay = jnp.exp(jnp.where(causal, gap, -jnp.inf))
                mg = decay * gram[:, side * length : (side + 1) * length]
                dt = cols[:, h + HEADS : h + HEADS + 1]
                q_sum = q_sum + mg * dt
                raw = mg * k_st
                rows_ref[k, h : h + 1, :] = jnp.sum(raw * dt, axis=0, keepdims=True)
                result = jnp.where(place == h, jnp.sum(raw, axis=1, keepdims=True), result)
                weights.append((decay * k_st).astype(BF16))
            z2 = dot(jnp.concatenate(weights, axis=1), g_both, 1, 0)
            z_in = dot(b, f2, 1, 0) * end2
            dx_ref[:, wide] = (dt2 * (z2 + z_in)).astype(dx_ref.dtype)
            y_in = dot(c, e2, 1, 0) * grow2
            xz, gy = x2f * z_in, g2f * y_in
            zero = jnp.zeros_like(xz)
            for side in range(2):
                h = j + side
                mask = low if side == 0 else jnp.logical_not(low)
                xs = jnp.sum(jnp.where(mask, xz, zero), axis=1, keepdims=True)
                gs = jnp.sum(jnp.where(mask, gy, zero), axis=1, keepdims=True)
                result = jnp.where(place == h + heads, xs, result)
                result = jnp.where(place == h + 2 * heads, gs, result)
            ef_ref[k, :, lanes] = jnp.sum(
                e2.astype(F32) * f2.astype(F32), axis=0, keepdims=True
            )
            b_sum = b_sum + dot((x2f * (end2 * dt2)).astype(BF16), f2, 1, 1)
            c_sum = c_sum + dot((g2f * grow2).astype(BF16), e2, 1, 1)
        cols_ref[...] = result
        d_scores[...] = q_sum
        d_b[...] = b_sum
        d_c[...] = c_sum

    def step(t, unused):
        kf = t - z

        @pl.when(jnp.logical_and(kf >= 0, kf < chunks))
        def _():
            copy_s(kf).wait_recv()
            pl.when(jnp.logical_not(first))(lambda: copy_e(kf).wait_recv())
            advance(kf, s_ref, s_in, e_in, e_out, e_snd, odd == 0)
            pl.when(jnp.logical_not(last))(lambda: copy_e(kf).start())

        kb = t - (nz - 1 - z)

        @pl.when(jnp.logical_and(kb >= 0, kb < chunks))
        def _():
            copy_a(kb).wait_recv()
            pl.when(jnp.logical_not(last))(lambda: copy_f(kb).wait_recv())
            advance(kb, a_ref, a_in, f_in, f_out, f_snd, odd == 1)
            pl.when(jnp.logical_not(first))(lambda: copy_f(kb).start())

        pl.when(t >= nz - 1)(lambda: gradients(t - (nz - 1)))
        return unused

    lax.fori_loop(0, chunks + nz - 1, step, 0)
    dk = d_scores[...].astype(BF16)
    gbc_ref[:, :state] = (d_b[...] + dot(dk, c, 1, 0)).astype(gbc_ref.dtype)
    gbc_ref[:, state:] = (d_c[...] + dot(dk, b, 0, 0)).astype(gbc_ref.dtype)
    copy_d().wait_send()

    def settle(k, unused):
        copy_s(k).wait_send()
        copy_a(k).wait_send()
        pl.when(jnp.logical_not(last))(lambda: copy_e(k).wait_send())
        pl.when(jnp.logical_not(first))(lambda: copy_f(k).wait_send())
        return unused

    lax.fori_loop(0, chunks, settle, 0)


def weight_kernel(
    n, m, t_ref, g_ref, rate_ref, out_ref, rate_out,
    acc, got, ring, r_acc, r_got, sem, out_sem, r_sem,
):
    chunks, blocks, rows = acc.shape[0], acc.shape[1], acc.shape[2]
    piece = chunks * rows
    seq, dp = lax.axis_index("seq"), lax.axis_index("dp")
    dp_steps, seq_steps, bit = [], [], 1
    while bit < m:
        dp_steps.append(("dp", bit, lax.rem(lax.div(dp, bit), 2)))
        bit *= 2
    bit = 1
    while bit < n:
        seq_steps.append(("seq", bit, lax.rem(lax.div(seq, bit), 2)))
        bit *= 2
    count = len(dp_steps) + len(seq_steps)
    orders = (dp_steps + seq_steps, dp_steps[:1] + seq_steps + dp_steps[1:])

    def peer(c, s):
        axis, bit, mine = orders[c % 2][s]
        return {axis: lax.axis_index(axis) + bit - 2 * bit * mine}

    def dp_peer(k):
        other, bit = dp, 1
        while bit < m:
            if k & bit:
                other = other + bit - 2 * bit * lax.rem(lax.div(dp, bit), 2)
            bit *= 2
        return {"dp": other}

    barrier = pltpu.get_barrier_semaphore()
    friends = [dp_peer(k) for k in range(1, m)] + [
        peer(0, s) for s in range(len(dp_steps), count)
    ]
    for friend in friends:
        pl.semaphore_signal(
            barrier, inc=1, device_id=friend, device_id_type=pl.DeviceIdType.MESH
        )

    starts, offsets = [], []
    for order in orders:
        base, width, total = 0, blocks, 0
        starts.append([])
        for unused, unused, mine in order:
            width //= 2
            starts[-1].append((base + width * mine, base + width * (1 - mine), width))
            base = base + width * mine
            if len(starts) == 1:
                offsets.append(total)
                total += width

    def copy(c, s):
        keep, give, size = starts[c % 2][s]
        return pltpu.make_async_remote_copy(
            src_ref=acc.at[c, pl.ds(give, size)],
            dst_ref=got.at[c, pl.ds(offsets[s], size)],
            send_sem=sem.at[0, c, s], recv_sem=sem.at[1, c, s],
            device_id=peer(c, s), device_id_type=pl.DeviceIdType.MESH,
        )

    def rate_copy(s):
        return pltpu.make_async_remote_copy(
            src_ref=r_acc.at[s], dst_ref=r_got.at[s],
            send_sem=r_sem.at[0, s], recv_sem=r_sem.at[1, s],
            device_id=peer(0, s), device_id_type=pl.DeviceIdType.MESH,
        )

    def out_copy(c, k):
        return pltpu.make_async_remote_copy(
            src_ref=ring.at[0, c], dst_ref=ring.at[k, c],
            send_sem=out_sem.at[0, c, k], recv_sem=out_sem.at[1, c, k],
            device_id=dp_peer(k), device_id_type=pl.DeviceIdType.MESH,
        )

    g = g_ref[...]
    r_acc[0] = rate_ref[...]
    block = 128
    for first in range(0, t_ref.shape[1], block):
        product = dot(t_ref[:, first : first + block], g, 0, 0)
        for part in range(0, block, rows):
            row = first + part
            owner, inner = row // (m * piece), row % (m * piece)
            chunk, place = inner % piece // rows, 0
            for axis, bit, unused in orders[chunk % 2]:
                index = inner // piece if axis == "dp" else owner
                place = 2 * place + index // bit % 2
            acc[chunk, place] = product[part : part + rows]
    pl.semaphore_wait(barrier, len(friends))
    for c in range(chunks):
        copy(c, 0).start()
    rate_copy(0).start()
    for s in range(count):
        for c in range(chunks):
            copy(c, s).wait_recv()
            keep, give, size = starts[c % 2][s]
            value = acc[c, pl.ds(keep, size)] + got[c, pl.ds(offsets[s], size)]
            if s + 1 < count:
                acc[c, pl.ds(keep, size)] = value
                copy(c, s + 1).start()
            else:
                ring[0, c] = value[0]
                for k in range(1, m):
                    out_copy(c, k).start()
        rate_copy(s).wait_recv()
        r_acc[s + 1] = r_acc[s] + r_got[s]
        if s + 1 < count:
            rate_copy(s + 1).start()
    rate_out[...] = r_acc[count]
    for c in range(chunks):
        for k in range(m):
            if k > 0:
                out_copy(c, k).wait_recv()
            where = dp_peer(k)["dp"] if k > 0 else dp
            out_ref[pl.ds(where * piece + c * rows, rows)] = ring[k, c]
    for c in range(chunks):
        for s in range(count):
            copy(c, s).wait_send()
        for k in range(1, m):
            out_copy(c, k).wait_send()
    for s in range(count):
        rate_copy(s).wait_send()


def shards(layer_input, projection, ssm_input, step_logit, decay_rate, output_grad):
    tokens, x_rows, logit, grad_rows = layer_input[0], ssm_input[0], step_logit[0], output_grad[0]
    length, full = x_rows.shape
    heads = logit.shape[1]
    size = full // heads
    state = projection.shape[1] // 2
    groups = heads // HEADS
    width = HEADS * size
    count = lax.axis_size("seq")
    projected = jnp.dot(tokens, projection, preferred_element_type=F32).astype(BF16)
    b_rows, c_rows = projected[:, :state], projected[:, state:]
    dt = jax.nn.softplus(logit)
    log_decay = jnp.cumsum(-decay_rate[None, :] * dt, axis=0)
    to_end = jnp.exp(log_decay[-1][None, :] - log_decay)
    grow = jnp.exp(log_decay)
    span = grow[-1]

    def by_group(value):
        return value.reshape(length, groups, HEADS).transpose(1, 0, 2)

    cols = jnp.concatenate([by_group(v) for v in (log_decay, dt, to_end, grow)], axis=2)
    span_rows = jnp.broadcast_to(
        jnp.broadcast_to(span.reshape(groups, 1, HEADS, 1), (groups, 1, HEADS, size)).reshape(
            groups, 1, width
        ),
        (groups, 8, width),
    )
    limit = 60 * 2**20
    vmem = pl.BlockSpec(memory_space=pltpu.VMEM)
    slots = pltpu.VMEM((groups, state, width), F32)
    half = pltpu.VMEM((groups, state, width), BF16)
    square = pltpu.VMEM((length, length), F32)
    sums = pltpu.VMEM((length, state), F32)
    grad_x, row_sums, col_sums, inner, grad_bc = pl.pallas_call(
        functools.partial(layer_kernel, count, size),
        in_specs=[vmem] * 7,
        out_specs=[vmem] * 5,
        out_shape=[
            jax.ShapeDtypeStruct((length, full), BF16),
            jax.ShapeDtypeStruct((groups, HEADS, length), F32),
            jax.ShapeDtypeStruct((length, 3 * heads), F32),
            jax.ShapeDtypeStruct((groups, 1, width), F32),
            jax.ShapeDtypeStruct((length, 2 * state), BF16),
        ],
        scratch_shapes=[slots, slots, half, half, square, square, sums, sums]
        + [pltpu.VMEM((groups, 8, width), F32)]
        + [slots] * 6
        + [pltpu.SemaphoreType.DMA((2, 1))]
        + [pltpu.SemaphoreType.DMA((2, groups))] * 4,
        compiler_params=pltpu.CompilerParams(
            collective_id=0, has_side_effects=True, vmem_limit_bytes=limit
        ),
        name="layer_gradients",
    )(
        b_rows, c_rows, x_rows, grad_rows, cols,
        log_decay.T.reshape(groups, HEADS, length), span_rows,
    )
    row_sums = row_sums.reshape(heads, length)
    inside, x_in, g_in = (col_sums[:, i * heads : (i + 1) * heads] for i in range(3))
    both = span * jnp.sum(inner.reshape(heads, size), axis=1)
    position = jnp.arange(length)
    earlier = (position[:, None] > position[None, :]).astype(F32)
    change = g_in + row_sums.T - dt * inside
    d_log = (
        both[None, :]
        + jnp.dot(earlier, dt * x_in, precision=lax.Precision.HIGHEST)
        + jnp.dot((position[:, None] <= position[None, :]).astype(F32), change, precision=lax.Precision.HIGHEST)
    )
    d_dt = inside + x_in - decay_rate[None, :] * d_log
    grad_logit = d_dt * jax.nn.sigmoid(logit)
    grad_rate = -jnp.sum(dt * d_log, axis=0)
    members = lax.axis_size("dp")
    blocks = count * members
    piece = tokens.shape[1] // blocks
    chunks = max(1, min(8, piece // 8))
    rows = piece // chunks
    levels = blocks.bit_length() - 1
    rate_rows = jnp.pad(grad_rate.reshape(1, heads), ((0, 7), (0, 128 - heads)))
    weight_rows, rate_sum = pl.pallas_call(
        functools.partial(weight_kernel, count, members),
        in_specs=[vmem] * 3,
        out_specs=[vmem] * 2,
        out_shape=[
            jax.ShapeDtypeStruct((members * piece, 2 * state), F32),
            jax.ShapeDtypeStruct((8, 128), F32),
        ],
        scratch_shapes=[
            pltpu.VMEM((chunks, blocks, rows, 2 * state), F32),
            pltpu.VMEM((chunks, blocks, rows, 2 * state), F32),
            pltpu.VMEM((members, chunks, rows, 2 * state), F32),
            pltpu.VMEM((levels + 1, 8, 128), F32),
            pltpu.VMEM((levels, 8, 128), F32),
            pltpu.SemaphoreType.DMA((2, chunks, levels)),
            pltpu.SemaphoreType.DMA((2, chunks, members)),
            pltpu.SemaphoreType.DMA((2, levels)),
        ],
        compiler_params=pltpu.CompilerParams(
            collective_id=1, has_side_effects=True, vmem_limit_bytes=limit
        ),
        name="weight_gradient",
    )(tokens, grad_bc, rate_rows)
    rate_sum = rate_sum[0, :heads]
    return (grad_x[None], grad_logit[None], rate_sum, weight_rows)


def solution(mesh):
    placed = (
        P("dp", "seq", None),
        P(),
        P("dp", "seq", None),
        P("dp", "seq", None),
        P(),
        P("dp", "seq", None),
    )
    return jax.shard_map(
        shards,
        mesh=mesh,
        in_specs=placed,
        out_specs=(P("dp", "seq", None), P("dp", "seq", None), P(), P("seq", None)),
        check_vma=False,
    )
```

profile of v0, /device:TPU:0, one launch (start us, length us, event | category | flops | bytes accessed | tf_op | source)
XLA Modules:
  0.0 170.1 jit_solution(18085267567905327624)
XLA Ops:
  0.6 0.0 copy-start
  0.6 0.0 copy-start.3
  0.7 0.8 neg.27
  1.5 0.8 copy.31
  2.4 0.2 reduce_window_sum.11
  2.6 0.1 broadcast_in_dim.12
  2.7 0.1 sub.17
  2.7 0.1 broadcast_in_dim.13
  2.8 0.1 broadcast_in_dim.14
  2.9 0.1 copy.32
  3.0 0.7 copy.33
  3.7 0.0 copy-done
  3.7 1.7 convolution_convert_fusion
  5.4 0.6 fusion.20
  6.0 0.0 copy-done.3
  6.0 0.1 exponential_bitcast_fusion.1
  6.1 0.7 broadcast_in_dim.30.d_ref
  6.8 1.3 copy.34.col_ref
  8.1 0.0 copy-start.4
  8.1 115.6 %layer_gradients.1 = (bf16[128,4096]{1,0:T(8,128)(2,1)}, f32[16,4,128]{2,1,0:T(4,128)}, f32[128,192]{1,0:T(8,128)}, f32[16,1,256]{2,1,0:T(1,128)}, bf16[128,256]{1,0:T(8,128)(2,1)}) custom-call(bf16[128,128]{1,0:T(8,128)(2,1)} %get-tuple-element.35.b_ref, bf16[128,128]{1,0:T(8,128)(2,1)} %get-tuple-element.34.c_ref, bf16[128,4096]{1,0:T(8,128)(2,1)} %bitcast.79, ...), custom_call_target="tpu_custom_call" | custom-call | tf_op jit(solution)/shard_map/layer_gradients/pallas_call | solution.py:391
  123.8 0.0 copy-start.1
  123.8 0.8 reduce.2
  124.6 0.1 reshape.53
  124.7 0.1 reduce_sum.20
  124.8 1.1 convolution_add_fusion.1
  125.9 0.8 copy.36
  126.8 0.0 copy-done.4
  126.8 1.2 multiply_reduce_fusion
  128.0 0.6 pad.4.rate_ref
  128.6 0.7 copy.38
  129.3 37.8 %weight_gradient.1 = (f32[512,256]{1,0:T(8,128)}, f32[8,128]{1,0:T(8,128)}) custom-call(bf16[128,4096]{1,0:T(8,128)(2,1)} %bitcast.78, bf16[128,256]{1,0:T(8,128)(2,1)} %get-tuple-element.15.g_ref, f32[8,128]{1,0:T(8,128)} %pad.4.rate_ref), custom_call_target="tpu_custom_call" | custom-call | tf_op jit(solution)/shard_map/weight_gradient/pallas_call | solution.py:436
  167.1 0.0 copy-start.2
  167.1 1.2 slice_bitcast_fusion
  168.4 0.0 copy-done.1
  168.4 1.0 copy.43
  169.3 0.0 copy-done.2
  169.3 0.8 copy.44
  (5 shorter events, 0.1 us)
Async XLA Ops:
  0.6 3.1 %copy-start = (bf16[4096,256]{1,0:T(8,128)(2,1)S(1)}, bf16[4096,256]{1,0:T(8,128)(2,1)}, u32[]{:S(2)}) copy-start(bf16[4096,256]{1,0:T(8,128)(2,1)} %param.7) | copy-start | bytes 6291460
  0.6 5.4 %copy-start.3 = (f32[1,128,64]{1,2,0:T(8,128)S(1)}, f32[1,128,64]{1,2,0:T(8,128)}, u32[]{:S(2)}) copy-start(f32[1,128,64]{1,2,0:T(8,128)} %param.9) | copy-start | bytes 98308
  8.1 118.7 %copy-start.4 = (f32[64]{0:T(128)S(1)}, f32[64]{0:T(128)}, u32[]{:S(2)}) copy-start(f32[64]{0:T(128)} %param.10) | copy-start | bytes 772
  123.8 44.6 %copy-start.1 = (bf16[128,4096]{1,0:T(8,128)(2,1)S(1)}, bf16[128,4096]{1,0:T(8,128)(2,1)}, u32[]{:S(2)}) copy-start(bf16[128,4096]{1,0:T(8,128)(2,1)} %get-tuple-element.11) | copy-start | bytes 3145732
  167.1 2.2 %copy-start.2 = (f32[512,256]{1,0:T(8,128)S(1)}, f32[512,256]{1,0:T(8,128)}, u32[]{:S(2)}) copy-start(f32[512,256]{1,0:T(8,128)} %get-tuple-element.46) | copy-start | bytes 1572868
where the time goes:
time: 171 us; the launch traced here: 170 us
  Pallas kernels  153 us (89%)
  local copies, waits for them, and re-layouts  9.86 us (6%)
  matrix products  4 us (2%)
  other arithmetic  2.12 us (1%)
    pallas_call x1, Pallas kernels, shards(): pl.pallas_call(functools.partial(layer_kernel, count, size), in_specs=[vm...  116 us
    pallas_call x1, Pallas kernels, shards(): pl.pallas_call(functools.partial(weight_kernel, count, members), in_specs...  37.8 us

commit v1 on v0

--- a/solution.py
+++ b/solution.py
@@ -23,16 +23,17 @@
 
 
 def layer_kernel(
-    n, size, b_ref, c_ref, x_ref, g_ref, col_ref, row_ref, d_ref,
+    n, size, b_ref, c_ref, cf_ref, x_ref, g_ref, col_ref, row_ref, d_ref,
     dx_ref, rows_ref, cols_ref, ef_ref, gbc_ref,
-    s_ref, a_ref, e_out, f_out, scores, d_scores, d_b, d_c,
-    d_in, s_in, a_in, e_in, f_in, e_snd, f_snd,
-    d_sem, s_sem, a_sem, e_sem, f_sem,
+    e_own, e_other, f_own, f_other, scores, d_scores, d_b, d_c, back, back_ef,
+    d_in, cf_in, c_in, gs_snd, gs_in, e_in, f_in, e_snd, f_snd, back_in, back_ef_in,
+    small_sem, gs_sem, e_sem, f_sem,
 ):
-    chunks = s_ref.shape[0]
+    chunks = gs_snd.shape[0]
     length = b_ref.shape[0]
     state = b_ref.shape[1]
     width = 2 * size
+    group = HEADS * size
     heads = chunks * HEADS
     nz = n // 2
     me = lax.axis_index("seq")
@@ -58,13 +59,19 @@
         )
 
     def copy_d():
-        return send(d_ref, d_in, d_sem, 0, partner)
-
-    def copy_s(k):
-        return send(s_ref.at[k], s_in.at[k], s_sem, k, partner)
-
-    def copy_a(k):
-        return send(a_ref.at[k], a_in.at[k], a_sem, k, partner)
+        return send(d_ref, d_in, small_sem, 0, partner)
+
+    def copy_c():
+        return send(cf_ref, cf_in, small_sem, 1, partner)
+
+    def copy_back():
+        return send(back, back_in, small_sem, 2, partner)
+
+    def copy_back_ef():
+        return send(back_ef, back_ef_in, small_sem, 3, partner)
+
+    def copy_g(k):
+        return send(gs_snd.at[k], gs_in.at[k], gs_sem, k, partner)
 
     def copy_e(k):
         return send(e_snd.at[k], e_in.at[k], e_sem, k, me + 2)
@@ -73,35 +80,24 @@
         return send(f_snd.at[k], f_in.at[k], f_sem, k, me - 2)
 
     def pair_lanes(k, pair):
-        return pl.ds(pl.multiple_of(k * (HEADS * size) + pair * width, width), width)
-
-    def local(k, unused):
+        return pl.ds(pl.multiple_of(k * group + pair * width, width), width)
+
+    def scale(k, unused):
         cols = col_ref[k]
         for pair in range(HEADS // 2):
-            lanes = pl.ds(pair * width, width)
-            wide = pair_lanes(k, pair)
-            j = 2 * pair
-            to_end = pair_columns(cols, j + HEADS, size) * pair_columns(cols, j + 2 * HEADS, size)
-            grow = pair_columns(cols, j + 3 * HEADS, size)
-            xs = (x_ref[:, wide].astype(F32) * to_end).astype(BF16)
-            gs = (g_ref[:, wide].astype(F32) * grow).astype(BF16)
-            s_ref[k, :, lanes] = dot(b_ref[...], xs, 0, 0)
-            a_ref[k, :, lanes] = dot(c_ref[...], gs, 0, 0)
-
-        @pl.when(k > 0)
-        def _():
-            copy_s(k - 1).start()
-            copy_a(k - 1).start()
-
+            grow = pair_columns(cols, 2 * pair + 3 * HEADS, size)
+            gs_snd[k, :, pl.ds(pair * width, width)] = (
+                g_ref[:, pair_lanes(k, pair)].astype(F32) * grow
+            )
+        copy_g(k).start()
         return unused
 
     end = jnp.logical_or(first, last)
     pl.when(end)(lambda: pl.semaphore_wait(barrier, min(nz, 2)))
     pl.when(jnp.logical_not(end))(lambda: pl.semaphore_wait(barrier, 3))
     copy_d().start()
-    lax.fori_loop(0, chunks, local, 0)
-    copy_s(chunks - 1).start()
-    copy_a(chunks - 1).start()
+    copy_c().start()
+    lax.fori_loop(0, chunks, scale, 0)
 
     @pl.when(first)
     def _():
@@ -116,22 +112,57 @@
     d_scores[...] = jnp.zeros_like(d_scores)
     d_b[...] = jnp.zeros_like(d_b)
     d_c[...] = jnp.zeros_like(d_c)
+    back[...] = jnp.zeros_like(back)
     cols_ref[...] = jnp.zeros_like(cols_ref)
     copy_d().wait_recv()
-
-    def advance(k, near, far, carry, out, snd, near_first):
-        @pl.when(near_first)
+    copy_c().wait_recv()
+    c_in[...] = cf_in[...].astype(BF16)
+
+    def row(ref, k):
+        return ref[k]
+
+    def forward(k):
+        cols = col_ref[k]
+        value = e_in[k]
+        parts = []
+        for pair in range(HEADS // 2):
+            j = 2 * pair
+            weight = pair_columns(cols, j + HEADS, size) * pair_columns(cols, j + 2 * HEADS, size)
+            parts.append((x_ref[:, pair_lanes(k, pair)].astype(F32) * weight).astype(BF16))
+        near = dot(b_ref[...], jnp.concatenate(parts, axis=1), 0, 0)
+
+        @pl.when(odd == 0)
         def _():
-            value = carry[k]
-            out[k] = value.astype(out.dtype)
-            middle = d_ref[k, 0:1] * value + near[k]
-            snd[k] = d_in[k, 0:1] * middle + far[k]
-
-        @pl.when(jnp.logical_not(near_first))
+            e_own[k] = value.astype(BF16)
+            middle = row(d_ref, k) * value + near
+            e_other[k] = middle.astype(BF16)
+            e_snd[k] = row(d_in, k) * middle
+
+        @pl.when(odd == 1)
         def _():
-            middle = d_in[k, 0:1] * carry[k] + far[k]
-            out[k] = middle.astype(out.dtype)
-            snd[k] = d_ref[k, 0:1] * middle + near[k]
+            e_other[k] = value.astype(BF16)
+            middle = row(d_in, k) * value
+            e_own[k] = middle.astype(BF16)
+            e_snd[k] = row(d_ref, k) * middle + near
+
+    def backward(k):
+        value = f_in[k]
+        near = dot(c_ref[...], gs_snd[k].astype(BF16), 0, 0)
+        far = dot(c_in[...], gs_in[k].astype(BF16), 0, 0)
+
+        @pl.when(odd == 0)
+        def _():
+            f_other[k] = value.astype(BF16)
+            middle = row(d_in, k) * value + far
+            f_own[k] = middle.astype(BF16)
+            f_snd[k] = row(d_ref, k) * middle + near
+
+        @pl.when(odd == 1)
+        def _():
+            f_own[k] = value.astype(BF16)
+            middle = row(d_ref, k) * value + near
+            f_other[k] = middle.astype(BF16)
+            f_snd[k] = row(d_in, k) * middle + far
 
     def gradients(k):
         cols = col_ref[k]
@@ -142,19 +173,22 @@
         )
         low = lax.broadcasted_iota(jnp.int32, (length, width), 1) < size
         place = lax.broadcasted_iota(jnp.int32, cols_ref.shape, 1) - k * HEADS
+        other_place = lax.broadcasted_iota(jnp.int32, (length, state), 1) - k * HEADS
         result = cols_ref[...]
+        other = back[1]
         q_sum = d_scores[...]
-        b_sum, c_sum = d_b[...], d_c[...]
+        b_sum, c_sum, c_other = d_b[...], d_c[...], back[0]
         for pair in range(HEADS // 2):
             lanes = pl.ds(pair * width, width)
             wide = pair_lanes(k, pair)
             x2, g2 = x_ref[:, wide], g_ref[:, wide]
-            x2f, g2f = x2.astype(F32), g2.astype(F32)
-            e2, f2 = e_out[k, :, lanes], f_out[k, :, lanes]
+            x2f = x2.astype(F32)
+            e2, f2 = e_own[k, :, lanes], f_own[k, :, lanes]
+            e2o, f2o = e_other[k, :, lanes], f_other[k, :, lanes]
+            gs, gso = gs_snd[k, :, lanes], gs_in[k, :, lanes]
             j = 2 * pair
             dt2 = pair_columns(cols, j + HEADS, size)
             end2 = pair_columns(cols, j + 2 * HEADS, size)
-            grow2 = pair_columns(cols, j + 3 * HEADS, size)
             g_low = jnp.where(low, g2, jnp.zeros_like(g2))
             g_high = jnp.where(low, jnp.zeros_like(g2), g2)
             g_both = jnp.concatenate([g_low, g_high], axis=0)
@@ -174,57 +208,74 @@
             z2 = dot(jnp.concatenate(weights, axis=1), g_both, 1, 0)
             z_in = dot(b, f2, 1, 0) * end2
             dx_ref[:, wide] = (dt2 * (z2 + z_in)).astype(dx_ref.dtype)
-            y_in = dot(c, e2, 1, 0) * grow2
-            xz, gy = x2f * z_in, g2f * y_in
+            xz = x2f * z_in
+            gy = gs * dot(c, e2, 1, 0)
+            gyo = gso * dot(c_in[...], e2o, 1, 0)
             zero = jnp.zeros_like(xz)
             for side in range(2):
                 h = j + side
                 mask = low if side == 0 else jnp.logical_not(low)
                 xs = jnp.sum(jnp.where(mask, xz, zero), axis=1, keepdims=True)
-                gs = jnp.sum(jnp.where(mask, gy, zero), axis=1, keepdims=True)
+                ys = jnp.sum(jnp.where(mask, gy, zero), axis=1, keepdims=True)
+                yo = jnp.sum(jnp.where(mask, gyo, zero), axis=1, keepdims=True)
                 result = jnp.where(place == h + heads, xs, result)
-                result = jnp.where(place == h + 2 * heads, gs, result)
+                result = jnp.where(place == h + 2 * heads, ys, result)
+                other = jnp.where(other_place == h, yo, other)
             ef_ref[k, :, lanes] = jnp.sum(
                 e2.astype(F32) * f2.astype(F32), axis=0, keepdims=True
             )
+            back_ef[k, :, lanes] = jnp.sum(
+                e2o.astype(F32) * f2o.astype(F32), axis=0, keepdims=True
+            )
             b_sum = b_sum + dot((x2f * (end2 * dt2)).astype(BF16), f2, 1, 1)
-            c_sum = c_sum + dot((g2f * grow2).astype(BF16), e2, 1, 1)
+            c_sum = c_sum + dot(gs.astype(BF16), e2, 1, 1)
+            c_other = c_other + dot(gso.astype(BF16), e2o, 1, 1)
         cols_ref[...] = result
+        back[1] = other
         d_scores[...] = q_sum
         d_b[...] = b_sum
         d_c[...] = c_sum
+        back[0] = c_other
 
     def step(t, unused):
         kf = t - z
 
         @pl.when(jnp.logical_and(kf >= 0, kf < chunks))
         def _():
-            copy_s(kf).wait_recv()
             pl.when(jnp.logical_not(first))(lambda: copy_e(kf).wait_recv())
-            advance(kf, s_ref, s_in, e_in, e_out, e_snd, odd == 0)
+            forward(kf)
             pl.when(jnp.logical_not(last))(lambda: copy_e(kf).start())
 
         kb = t - (nz - 1 - z)
 
         @pl.when(jnp.logical_and(kb >= 0, kb < chunks))
         def _():
-            copy_a(kb).wait_recv()
+            copy_g(kb).wait_recv()
             pl.when(jnp.logical_not(last))(lambda: copy_f(kb).wait_recv())
-            advance(kb, a_ref, a_in, f_in, f_out, f_snd, odd == 1)
+            backward(kb)
             pl.when(jnp.logical_not(first))(lambda: copy_f(kb).start())
 
         pl.when(t >= nz - 1)(lambda: gradients(t - (nz - 1)))
         return unused
 
     lax.fori_loop(0, chunks + nz - 1, step, 0)
+    copy_back().start()
+    copy_back_ef().start()
     dk = d_scores[...].astype(BF16)
     gbc_ref[:, :state] = (d_b[...] + dot(dk, c, 1, 0)).astype(gbc_ref.dtype)
-    gbc_ref[:, state:] = (d_c[...] + dot(dk, b, 0, 0)).astype(gbc_ref.dtype)
+    c_total = d_c[...] + dot(dk, b, 0, 0)
+    copy_back().wait_recv()
+    copy_back_ef().wait_recv()
+    gbc_ref[:, state:] = (c_total + back_in[0]).astype(gbc_ref.dtype)
+    cols_ref[:, 2 * heads :] += back_in[1, :, :heads]
+    ef_ref[...] += back_ef_in[...]
     copy_d().wait_send()
+    copy_c().wait_send()
+    copy_back().wait_send()
+    copy_back_ef().wait_send()
 
     def settle(k, unused):
-        copy_s(k).wait_send()
-        copy_a(k).wait_send()
+        copy_g(k).wait_send()
         pl.when(jnp.logical_not(last))(lambda: copy_e(k).wait_send())
         pl.when(jnp.logical_not(first))(lambda: copy_f(k).wait_send())
         return unused
@@ -367,7 +418,9 @@
     projected = jnp.dot(tokens, projection, preferred_element_type=F32).astype(BF16)
     b_rows, c_rows = projected[:, :state], projected[:, state:]
     dt = jax.nn.softplus(logit)
-    log_decay = jnp.cumsum(-decay_rate[None, :] * dt, axis=0)
+    position = jnp.arange(length)
+    until = (position[:, None] >= position[None, :]).astype(F32)
+    log_decay = jnp.dot(until, -decay_rate[None, :] * dt, precision=lax.Precision.HIGHEST)
     to_end = jnp.exp(log_decay[-1][None, :] - log_decay)
     grow = jnp.exp(log_decay)
     span = grow[-1]
@@ -376,12 +429,7 @@
         return value.reshape(length, groups, HEADS).transpose(1, 0, 2)
 
     cols = jnp.concatenate([by_group(v) for v in (log_decay, dt, to_end, grow)], axis=2)
-    span_rows = jnp.broadcast_to(
-        jnp.broadcast_to(span.reshape(groups, 1, HEADS, 1), (groups, 1, HEADS, size)).reshape(
-            groups, 1, width
-        ),
-        (groups, 8, width),
-    )
+    span_rows = jnp.broadcast_to(span[:, None], (heads, size)).reshape(groups, 1, width)
     limit = 60 * 2**20
     vmem = pl.BlockSpec(memory_space=pltpu.VMEM)
     slots = pltpu.VMEM((groups, state, width), F32)
@@ -390,7 +438,7 @@
     sums = pltpu.VMEM((length, state), F32)
     grad_x, row_sums, col_sums, inner, grad_bc = pl.pallas_call(
         functools.partial(layer_kernel, count, size),
-        in_specs=[vmem] * 7,
+        in_specs=[vmem] * 8,
         out_specs=[vmem] * 5,
         out_shape=[
             jax.ShapeDtypeStruct((length, full), BF16),
@@ -399,23 +447,25 @@
             jax.ShapeDtypeStruct((groups, 1, width), F32),
             jax.ShapeDtypeStruct((length, 2 * state), BF16),
         ],
-        scratch_shapes=[slots, slots, half, half, square, square, sums, sums]
-        + [pltpu.VMEM((groups, 8, width), F32)]
-        + [slots] * 6
-        + [pltpu.SemaphoreType.DMA((2, 1))]
-        + [pltpu.SemaphoreType.DMA((2, groups))] * 4,
+        scratch_shapes=[half] * 4 + [square, square, sums, sums]
+        + [pltpu.VMEM((2, length, state), F32), pltpu.VMEM((groups, 1, width), F32)]
+        + [pltpu.VMEM((groups, 1, width), F32), sums, pltpu.VMEM((length, state), BF16)]
+        + [pltpu.VMEM((groups, length, width), F32)] * 2
+        + [slots] * 4
+        + [pltpu.VMEM((2, length, state), F32), pltpu.VMEM((groups, 1, width), F32)]
+        + [pltpu.SemaphoreType.DMA((2, 4))]
+        + [pltpu.SemaphoreType.DMA((2, groups))] * 3,
         compiler_params=pltpu.CompilerParams(
             collective_id=0, has_side_effects=True, vmem_limit_bytes=limit
         ),
         name="layer_gradients",
     )(
-        b_rows, c_rows, x_rows, grad_rows, cols,
+        b_rows, c_rows, c_rows.astype(F32), x_rows, grad_rows, cols,
         log_decay.T.reshape(groups, HEADS, length), span_rows,
     )
     row_sums = row_sums.reshape(heads, length)
     inside, x_in, g_in = (col_sums[:, i * heads : (i + 1) * heads] for i in range(3))
     both = span * jnp.sum(inner.reshape(heads, size), axis=1)
-    position = jnp.arange(length)
     earlier = (position[:, None] > position[None, :]).astype(F32)
     change = g_in + row_sums.T - dt * inside
     d_log = (

time: 171 us -> 156 us (0.912)
  Pallas kernels: 153 us -> 139 us
    pallas_call x1, Pallas kernels: 116 us -> 101 us  [shards(): pl.pallas_call(functools.partial(layer_kernel, count, size), in_specs=[vm...]
where the time goes in v1:
time: 156 us
  Pallas kernels  139 us (89%)
  local copies, waits for them, and re-layouts  8.74 us (6%)
  matrix products  4.26 us (3%)
  other arithmetic  3.53 us (2%)
    pallas_call x1, Pallas kernels, shards(): pl.pallas_call(functools.partial(layer_kernel, count, size), in_specs=[vm...  101 us
    pallas_call x1, Pallas kernels, shards(): pl.pallas_call(functools.partial(weight_kernel, count, members), in_specs...  37.9 us
    unnamed x14, local copies, waits for them, and re-layouts  3.34 us

profile of v1, /device:TPU:0, one launch (start us, length us, event | category | flops | bytes accessed | tf_op | source)
XLA Modules:
  0.0 155.9 jit_solution(5691029414089496068)
XLA Ops:
  0.6 0.0 copy-start
  0.6 0.8 neg.27
  1.5 0.8 fusion.18
  2.3 0.8 copy.30
  3.1 0.3 fusion.14
  3.4 0.0 copy-start.2
  3.4 0.2 slice_reduce_fusion
  3.6 0.1 subtract_exponential_fusion
  3.7 0.2 slice_reduce_fusion.1
  3.8 0.1 broadcast_in_dim.10
  3.9 0.1 broadcast_in_dim.11
  4.0 0.7 broadcast_in_dim.12.d_ref
  4.8 0.0 copy-done
  4.8 1.7 %convolution_convert_fusion = bf16[128,256]{1,0:T(8,128)(2,1)S(1)} fusion(bf16[4096,256]{1,0:T(8,128)(2,1)S(1)} %copy-done, bf16[1,128,4096]{2,1,0:T(8,128)(2,1)} %param.6), kind=kOutput, calls=%fused_computation | convolution fusion | flops 268468224 | bytes 3211264 | tf_op jit(solution)/shard_map/dot_general | solution.py:418
  6.4 0.7 slice_convert_fusion
  7.1 1.3 copy.31.col_ref
  8.4 0.0 copy-done.2
  8.4 0.0 copy-start.4
  8.4 100.7 %layer_gradients.1 = (bf16[128,4096]{1,0:T(8,128)(2,1)}, f32[16,4,128]{2,1,0:T(4,128)}, f32[128,192]{1,0:T(8,128)}, f32[16,1,256]{2,1,0:T(1,128)}, bf16[128,256]{1,0:T(8,128)(2,1)}) custom-call(bf16[128,128]{1,0:T(8,128)(2,1)} %get-tuple-element.34.b_ref, bf16[128,128]{1,0:T(8,128)(2,1)} %get-tuple-element.33.c_ref, f32[128,128]{1,0:T(8,128)} %get-tuple-element.32.cf_ref, ...), custom_call_target="tpu_custom_call" | custom-call | tf_op jit(solution)/shard_map/layer_gradients/pallas_call | solution.py:439
  109.1 0.0 copy-start.1
  109.1 0.8 reduce.2
  110.0 0.1 reshape.55
  110.1 0.1 reduce_sum.20
  110.2 0.1 copy.32
  110.3 0.2 multiply_reduce_fusion.1
  110.5 1.1 convolution_add_fusion.1
  111.6 0.8 copy.34
  112.4 0.0 copy-done.4
  112.4 1.2 multiply_reduce_fusion
  113.7 0.6 pad.4.rate_ref
  114.3 0.7 copy.36
  115.0 37.9 %weight_gradient.1 = (f32[512,256]{1,0:T(8,128)}, f32[8,128]{1,0:T(8,128)}) custom-call(bf16[128,4096]{1,0:T(8,128)(2,1)} %bitcast.77, bf16[128,256]{1,0:T(8,128)(2,1)} %get-tuple-element.15.g_ref, f32[8,128]{1,0:T(8,128)} %pad.4.rate_ref), custom_call_target="tpu_custom_call" | custom-call | tf_op jit(solution)/shard_map/weight_gradient/pallas_call | solution.py:486
  152.8 0.0 copy-start.3
  152.8 1.2 slice_bitcast_fusion
  154.1 0.0 copy-done.1
  154.1 1.0 copy.41
  155.1 0.0 copy-done.3
  155.1 0.8 copy.42
  (2 shorter events, 0.0 us)
Async XLA Ops:
  0.6 4.1 %copy-start = (bf16[4096,256]{1,0:T(8,128)(2,1)S(1)}, bf16[4096,256]{1,0:T(8,128)(2,1)}, u32[]{:S(2)}) copy-start(bf16[4096,256]{1,0:T(8,128)(2,1)} %param.7) | copy-start | bytes 6291460
  3.4 5.0 %copy-start.2 = (f32[128,64]{0,1:T(8,128)}, f32[128,64]{0,1:T(8,128)S(1)}, u32[]{:S(2)}) copy-start(f32[128,64]{0,1:T(8,128)S(1)} %fusion.14) | copy-start | bytes 98308
  8.4 104.0 %copy-start.4 = (f32[64]{0:T(128)S(1)}, f32[64]{0:T(128)}, u32[]{:S(2)}) copy-start(f32[64]{0:T(128)} %param.10) | copy-start | bytes 772
  109.1 45.0 %copy-start.1 = (bf16[128,4096]{1,0:T(8,128)(2,1)S(1)}, bf16[128,4096]{1,0:T(8,128)(2,1)}, u32[]{:S(2)}) copy-start(bf16[128,4096]{1,0:T(8,128)(2,1)} %get-tuple-element.11) | copy-start | bytes 3145732
  152.8 2.2 %copy-start.3 = (f32[512,256]{1,0:T(8,128)S(1)}, f32[512,256]{1,0:T(8,128)}, u32[]{:S(2)}) copy-start(f32[512,256]{1,0:T(8,128)} %get-tuple-element.44) | copy-start | bytes 1572868

commit v2 on v1

--- a/solution.py
+++ b/solution.py
@@ -9,7 +9,8 @@
 
 F32 = jnp.float32
 BF16 = jnp.bfloat16
-HEADS = 4
+HEADS = 2
+LAG = 3
 
 
 def dot(a, b, ca, cb):
@@ -238,7 +239,7 @@
         back[0] = c_other
 
     def step(t, unused):
-        kf = t - z
+        kf = t - LAG * z
 
         @pl.when(jnp.logical_and(kf >= 0, kf < chunks))
         def _():
@@ -246,7 +247,7 @@
             forward(kf)
             pl.when(jnp.logical_not(last))(lambda: copy_e(kf).start())
 
-        kb = t - (nz - 1 - z)
+        kb = t - LAG * (nz - 1 - z)
 
         @pl.when(jnp.logical_and(kb >= 0, kb < chunks))
         def _():
@@ -255,10 +256,12 @@
             backward(kb)
             pl.when(jnp.logical_not(first))(lambda: copy_f(kb).start())
 
-        pl.when(t >= nz - 1)(lambda: gradients(t - (nz - 1)))
+        kg = t - delay
+        pl.when(jnp.logical_and(kg >= 0, kg < chunks))(lambda: gradients(kg))
         return unused
 
-    lax.fori_loop(0, chunks + nz - 1, step, 0)
+    delay = LAG * lax.max(z, nz - 1 - z)
+    lax.fori_loop(0, chunks + delay, step, 0)
     copy_back().start()
     copy_back_ef().start()
     dk = d_scores[...].astype(BF16)

time: 156 us -> 130 us (0.83)
  Pallas kernels: 139 us -> 111 us
  local copies, waits for them, and re-layouts: 8.74 us -> 10.4 us
    pallas_call x1, Pallas kernels: 101 us -> 74.4 us  [shards(): pl.pallas_call(functools.partial(layer_kernel, count, size), in_specs=[vm...]
    unnamed x14 -> x16, local copies, waits for them, and re-layouts: 3.34 us -> 3.89 us
where the time goes in v2:
time: 130 us
  Pallas kernels  111 us (85%)
  local copies, waits for them, and re-layouts  10.4 us (8%)
  other arithmetic  4.01 us (3%)
  matrix products  3.02 us (2%)
    pallas_call x1, Pallas kernels, shards(): pl.pallas_call(functools.partial(layer_kernel, count, size), in_specs=[vm...  74.4 us
    pallas_call x1, Pallas kernels, shards(): pl.pallas_call(functools.partial(weight_kernel, count, members), in_specs...  37.1 us
    unnamed x16, local copies, waits for them, and re-layouts  3.89 us

profile of v2, /device:TPU:0, one launch (start us, length us, event | category | flops | bytes accessed | tf_op | source)
XLA Modules:
  0.0 129.7 jit_solution(5599527644231855273)
XLA Ops:
  0.6 0.0 copy-start
  0.6 0.0 copy-start.1
  0.7 1.0 copy.30
  1.7 0.7 neg.27
  2.3 0.2 fusion.14
  2.6 0.0 copy-start.3
  2.6 0.2 slice_reduce_fusion
  2.8 0.1 subtract_exponential_fusion
  2.9 0.8 fusion.18
  3.7 0.1 pad_maximum_fusion
  3.8 2.0 %copy.31.col_ref = f32[32,128,8]{2,1,0:T(8,128)} copy(f32[32,128,8]{1,2,0:T(8,128)S(1)} %pad_maximum_fusion) | data formatting | bytes 262144 | tf_op jit(solution)/shard_map/concatenate | solution.py:434
  5.7 0.2 slice_reduce_fusion.1
  5.9 0.1 broadcast_in_dim.10
  6.0 0.1 broadcast_in_dim.11
  6.1 0.7 broadcast_in_dim.12.d_ref
  6.8 0.0 copy-done
  6.8 0.0 copy-done.1
  6.8 0.4 convolution_convert_fusion
  7.3 0.0 copy-done.3
  7.3 0.7 slice_convert_fusion
  7.9 0.0 copy-start.5
  8.0 74.4 %layer_gradients.1 = (bf16[128,4096]{1,0:T(8,128)(2,1)}, f32[32,2,128]{2,1,0:T(2,128)}, f32[128,192]{1,0:T(8,128)}, f32[32,1,128]{2,1,0:T(1,128)}, bf16[128,256]{1,0:T(8,128)(2,1)}) custom-call(bf16[128,128]{1,0:T(8,128)(2,1)} %get-tuple-element.34.b_ref, bf16[128,128]{1,0:T(8,128)(2,1)} %get-tuple-element.33.c_ref, f32[128,128]{1,0:T(8,128)} %get-tuple-element.32.cf_ref, ...), custom_call_target="tpu_custom_call" | custom-call | tf_op jit(solution)/shard_map/layer_gradients/pallas_call | solution.py:442
  82.4 0.0 copy-start.2
  82.4 0.5 broadcast.20
  82.9 1.4 %reduce.9 = f32[32,128]{1,0:T(8,128)S(1)} reduce(f32[32,1,128]{2,1,0:T(1,128)} %get-tuple-element.13, f32[]{:T(128)} %broadcast.20), dimensions={1}, to_apply=%get-tuple-element.13.reduce_sub_computation.3 | reduce | bytes 32772 | tf_op jit(solution)/shard_map/layer_gradients/pallas_call | solution.py:442
  84.3 0.1 reshape.55
  84.4 0.1 reduce_sum.20
  84.5 0.1 copy.32
  84.6 0.2 multiply_reduce_fusion.1
  84.8 1.1 convolution_add_fusion.1
  85.9 0.8 copy.34
  86.7 0.0 copy-done.5
  86.7 1.2 multiply_reduce_fusion
  88.0 0.6 pad.4.rate_ref
  88.6 37.1 %weight_gradient.1 = (f32[512,256]{1,0:T(8,128)}, f32[8,128]{1,0:T(8,128)}) custom-call(bf16[128,4096]{1,0:T(8,128)(2,1)} %bitcast.77, bf16[128,256]{1,0:T(8,128)(2,1)} %get-tuple-element.15.g_ref, f32[8,128]{1,0:T(8,128)} %pad.4.rate_ref), custom_call_target="tpu_custom_call" | custom-call | tf_op jit(solution)/shard_map/weight_gradient/pallas_call | solution.py:489
  125.7 1.2 slice_bitcast_fusion
  126.9 0.7 copy.36
  127.5 0.0 copy-start.4
  127.6 0.0 copy-done.2
  127.6 1.0 copy.41
  128.5 0.4 copy-done.4
  128.9 0.8 copy.42
  (1 shorter events, 0.0 us)
Async XLA Ops:
  0.6 6.2 %copy-start = (bf16[4096,256]{1,0:T(8,128)(2,1)S(1)}, bf16[4096,256]{1,0:T(8,128)(2,1)}, u32[]{:S(2)}) copy-start(bf16[4096,256]{1,0:T(8,128)(2,1)} %param.7) | copy-start | bytes 6291460
  0.6 6.2 %copy-start.1 = (bf16[1,128,4096]{2,1,0:T(8,128)(2,1)S(1)}, bf16[1,128,4096]{2,1,0:T(8,128)(2,1)}, u32[]{:S(2)}) copy-start(bf16[1,128,4096]{2,1,0:T(8,128)(2,1)} %param.6) | copy-start | bytes 3145732
  2.6 4.7 %copy-start.3 = (f32[128,64]{0,1:T(8,128)}, f32[128,64]{0,1:T(8,128)S(1)}, u32[]{:S(2)}) copy-start(f32[128,64]{0,1:T(8,128)S(1)} %fusion.14) | copy-start | bytes 98308
  7.9 78.8 %copy-start.5 = (f32[64]{0:T(128)S(1)}, f32[64]{0:T(128)}, u32[]{:S(2)}) copy-start(f32[64]{0:T(128)} %param.10) | copy-start | bytes 772
  82.4 45.2 %copy-start.2 = (bf16[128,4096]{1,0:T(8,128)(2,1)S(1)}, bf16[128,4096]{1,0:T(8,128)(2,1)}, u32[]{:S(2)}) copy-start(bf16[128,4096]{1,0:T(8,128)(2,1)} %get-tuple-element.11) | copy-start | bytes 3145732
  127.5 1.4 %copy-start.4 = (f32[512,256]{1,0:T(8,128)S(1)}, f32[512,256]{1,0:T(8,128)}, u32[]{:S(2)}) copy-start(f32[512,256]{1,0:T(8,128)} %get-tuple-element.44) | copy-start | bytes 1572868

commit v3 on v2

v3 whole, which is shorter than its diff:
```python
import functools

import jax
import jax.numpy as jnp
from jax import lax
from jax.experimental import pallas as pl
from jax.experimental.pallas import tpu as pltpu
from jax.sharding import PartitionSpec as P

F32 = jnp.float32
BF16 = jnp.bfloat16
HEADS = 2
LAG = 3
EARLY = 3


def dot(a, b, ca, cb):
    return lax.dot_general(a, b, (((ca,), (cb,)), ((), ())), preferred_element_type=F32)


def exact_dot(a, b, ca, cb):
    return lax.dot_general(
        a, b, (((ca,), (cb,)), ((), ())),
        preferred_element_type=F32, precision=lax.Precision.HIGHEST,
    )


def pair_columns(cols, j, size):
    lane = lax.broadcasted_iota(jnp.int32, (cols.shape[0], 2 * size), 1)
    return jnp.where(lane < size, cols[:, j : j + 1], cols[:, j + 1 : j + 2])


def layer_kernel(
    n, size, t_ref, w_ref, x_ref, g_ref, logit_ref, rate_ref,
    dx_ref, dlogit_ref, drate_ref, gbc_ref,
    b_ref, c_ref, c_in, cols1, cols2, rows_ref, span, span_in, cf, cf_in,
    e_own, e_other, f_own, f_other, scores, d_scores, d_b, d_c,
    sums1, sums2, row_sums, back, back_in,
    gs_snd, gs_in, e_in, f_in, e_snd, f_snd,
    small_sem, gs_sem, e_sem, f_sem,
):
    chunks = gs_snd.shape[0]
    length, state = b_ref.shape
    heads = logit_ref.shape[1]
    width = HEADS * size
    nz = n // 2
    me = lax.axis_index("seq")
    odd = lax.rem(me, 2)
    z = lax.div(me, 2)
    partner = me + 1 - 2 * odd
    first, last = z == 0, z == nz - 1
    barrier = pltpu.get_barrier_semaphore()

    def greet(who):
        pl.semaphore_signal(
            barrier, inc=1, device_id={"seq": who}, device_id_type=pl.DeviceIdType.MESH
        )

    greet(partner)
    pl.when(jnp.logical_not(first))(lambda: greet(me - 2))
    pl.when(jnp.logical_not(last))(lambda: greet(me + 2))

    def send(src, dst, sems, k, who):
        return pltpu.make_async_remote_copy(
            src_ref=src, dst_ref=dst, send_sem=sems.at[0, k], recv_sem=sems.at[1, k],
            device_id={"seq": who}, device_id_type=pl.DeviceIdType.MESH,
        )

    def copy_span():
        return send(span, span_in, small_sem, 0, partner)

    def copy_c():
        return send(cf, cf_in, small_sem, 1, partner)

    def copy_back(i):
        return send(back.at[i], back_in.at[i], small_sem, 2 + i, partner)

    def copy_g(k):
        return send(gs_snd.at[k], gs_in.at[k], gs_sem, k, partner)

    def copy_e(k):
        return send(e_snd.at[k], e_in.at[k], e_sem, k, me + 2)

    def copy_f(k):
        return send(f_snd.at[k], f_in.at[k], f_sem, k, me - 2)

    def turn(value, k):
        lanes = value.shape[1]
        return pltpu.roll(value, lax.rem(lanes - HEADS * k, lanes), 1)

    def wide(k):
        return pl.ds(pl.multiple_of(k * width, width), width)

    logit, rate = logit_ref[...], rate_ref[...]
    dt_all = jnp.maximum(logit, 0.0) + jnp.log1p(jnp.exp(-jnp.abs(logit)))
    row_at = lax.broadcasted_iota(jnp.int32, (length, length), 0)
    col_at = lax.broadcasted_iota(jnp.int32, (length, length), 1)
    until = (row_at >= col_at).astype(F32)
    log_decay = exact_dot(until, -rate * dt_all, 1, 0)
    to_end = jnp.exp(log_decay[length - 1 : length, :] - log_decay)
    grow_all = jnp.exp(log_decay)
    q1 = jnp.concatenate([log_decay, dt_all], axis=1)
    q2 = jnp.concatenate([to_end, grow_all], axis=1)
    span[...] = jnp.broadcast_to(q2[length - 1 : length, :], span.shape)
    by_head = q1.T
    for k in range(chunks):
        rows_ref[k] = by_head[HEADS * k : HEADS * (k + 1), :]

    def scale(k, unused):
        cols1[k] = turn(q1, k)
        cols = turn(q2, k)
        cols2[k] = cols
        gs_snd[k] = g_ref[:, wide(k)].astype(F32) * pair_columns(cols, heads, size)
        copy_g(k).start()
        return unused

    end = jnp.logical_or(first, last)
    pl.when(end)(lambda: pl.semaphore_wait(barrier, min(nz, 2)))
    pl.when(jnp.logical_not(end))(lambda: pl.semaphore_wait(barrier, 3))
    copy_span().start()
    lax.fori_loop(0, EARLY, scale, 0)
    bc = dot(t_ref[...], w_ref[...], 1, 0).astype(BF16)
    b_ref[...] = bc[:, :state]
    c_ref[...] = bc[:, state:]
    cf[...] = bc[:, state:].astype(F32)
    copy_c().start()
    lax.fori_loop(EARLY, chunks, scale, 0)

    @pl.when(first)
    def _():
        e_in[...] = jnp.zeros_like(e_in)

    @pl.when(last)
    def _():
        f_in[...] = jnp.zeros_like(f_in)

    scores[...] = dot(b_ref[...], c_ref[...], 1, 1)
    for ref in (d_scores, d_b, d_c, sums1, sums2, row_sums, back):
        ref[...] = jnp.zeros_like(ref)
    copy_span().wait_recv()
    copy_c().wait_recv()
    c_in[...] = cf_in[...].astype(BF16)

    def spans(ref, k):
        return pair_columns(turn(ref[...], k)[:1, :], heads, size)

    def forward(k):
        value = e_in[k]
        weight = pair_columns(cols1[k], heads, size) * pair_columns(cols2[k], 0, size)
        near = dot(b_ref[...], (x_ref[:, wide(k)].astype(F32) * weight).astype(BF16), 0, 0)
        mine, theirs = spans(span, k), spans(span_in, k)

        @pl.when(odd == 0)
        def _():
            e_own[k] = value.astype(BF16)
            middle = mine * value + near
            e_other[k] = middle.astype(BF16)
            e_snd[k] = theirs * middle

        @pl.when(odd == 1)
        def _():
            e_other[k] = value.astype(BF16)
            middle = theirs * value
            e_own[k] = middle.astype(BF16)
            e_snd[k] = mine * middle + near

    def backward(k):
        value = f_in[k]
        near = dot(c_ref[...], gs_snd[k].astype(BF16), 0, 0)
        far = dot(c_in[...], gs_in[k].astype(BF16), 0, 0)
        mine, theirs = spans(span, k), spans(span_in, k)

        @pl.when(odd == 0)
        def _():
            f_other[k] = value.astype(BF16)
            middle = theirs * value + far
            f_own[k] = middle.astype(BF16)
            f_snd[k] = mine * middle + near

        @pl.when(odd == 1)
        def _():
            f_own[k] = value.astype(BF16)
            middle = mine * value + near
            f_other[k] = middle.astype(BF16)
            f_snd[k] = theirs * middle + far

    def gradients(k):
        cols, rows = cols1[k], rows_ref[k]
        k_st = scores[...]
        causal = col_at >= row_at
        low = lax.broadcasted_iota(jnp.int32, (length, width), 1) < size
        place = lax.broadcasted_iota(jnp.int32, sums1.shape, 1) - k * HEADS
        row_place = lax.broadcasted_iota(jnp.int32, row_sums.shape, 0) - k * HEADS
        res1, res2, res3, res_rows = sums1[...], sums2[...], back[1], row_sums[...]
        q_sum = d_scores[...]
        x2, g2 = x_ref[:, wide(k)], g_ref[:, wide(k)]
        x2f = x2.astype(F32)
        e2, f2, e3, f3 = e_own[k], f_own[k], e_other[k], f_other[k]
        gs, gs3 = gs_snd[k], gs_in[k]
        dt2 = pair_columns(cols, heads, size)
        end2 = pair_columns(cols2[k], 0, size)
        g_low = jnp.where(low, g2, jnp.zeros_like(g2))
        g_high = jnp.where(low, jnp.zeros_like(g2), g2)
        g_both = jnp.concatenate([g_low, g_high], axis=0)
        gram = dot(x2, g_both, 1, 1)
        weights = []
        for h in range(HEADS):
            gap = rows[h : h + 1, :] - cols[:, h : h + 1]
            decay = jnp.exp(jnp.where(causal, gap, -jnp.inf))
            mg = decay * gram[:, h * length : (h + 1) * length]
            dt = cols[:, heads + h : heads + h + 1]
            q_sum = q_sum + mg * dt
            raw = mg * k_st
            res_rows = jnp.where(row_place == h, jnp.sum(raw * dt, axis=0, keepdims=True), res_rows)
            res1 = jnp.where(place == h, jnp.sum(raw, axis=1, keepdims=True), res1)
            weights.append((decay * k_st).astype(BF16))
        z2 = dot(jnp.concatenate(weights, axis=1), g_both, 1, 0)
        z_in = dot(b_ref[...], f2, 1, 0) * end2
        dx_ref[:, wide(k)] = (dt2 * (z2 + z_in)).astype(dx_ref.dtype)
        xz = x2f * z_in
        gy = gs * dot(c_ref[...], e2, 1, 0)
        gy3 = gs3 * dot(c_in[...], e3, 1, 0)
        ef = jnp.sum(e2.astype(F32) * f2.astype(F32), axis=0, keepdims=True)
        ef3 = jnp.sum(e3.astype(F32) * f3.astype(F32), axis=0, keepdims=True)
        low_row = low[:1, :]

        def half(value, h, mask):
            keep = mask if h == 0 else jnp.logical_not(mask)
            return jnp.sum(jnp.where(keep, value, jnp.zeros_like(value)), axis=1, keepdims=True)

        for h in range(HEADS):
            res1 = jnp.where(place == h + heads, half(xz, h, low), res1)
            res2 = jnp.where(place == h, half(gy, h, low), res2)
            res2 = jnp.where(place == h + heads, half(ef, h, low_row), res2)
            res3 = jnp.where(place == h, half(gy3, h, low), res3)
            res3 = jnp.where(place == h + heads, half(ef3, h, low_row), res3)
        sums1[...] = res1
        sums2[...] = res2
        back[1] = res3
        row_sums[...] = res_rows
        d_scores[...] = q_sum
        d_b[...] += dot((x2f * (end2 * dt2)).astype(BF16), f2, 1, 1)
        d_c[...] += dot(gs.astype(BF16), e2, 1, 1)
        back[0] += dot(gs3.astype(BF16), e3, 1, 1)

    delay = LAG * lax.max(z, nz - 1 - z)

    def step(t, unused):
        kf = t - LAG * z

        @pl.when(jnp.logical_and(kf >= 0, kf < chunks))
        def _():
            pl.when(jnp.logical_not(first))(lambda: copy_e(kf).wait_recv())
            forward(kf)
            pl.when(jnp.logical_not(last))(lambda: copy_e(kf).start())

        kb = t - LAG * (nz - 1 - z)

        @pl.when(jnp.logical_and(kb >= 0, kb < chunks))
        def _():
            copy_g(kb).wait_recv()
            pl.when(jnp.logical_not(last))(lambda: copy_f(kb).wait_recv())
            backward(kb)
            pl.when(jnp.logical_not(first))(lambda: copy_f(kb).start())

        kg = t - delay
        pl.when(jnp.logical_and(kg >= 0, kg < chunks))(lambda: gradients(kg))
        return unused

    lax.fori_loop(0, chunks + delay, step, 0)
    copy_back(0).start()
    copy_back(1).start()
    dk = d_scores[...].astype(BF16)
    gbc_ref[:, :state] = (d_b[...] + dot(dk, c_ref[...], 1, 0)).astype(gbc_ref.dtype)
    c_total = d_c[...] + dot(dk, b_ref[...], 0, 0)
    copy_back(0).wait_recv()
    gbc_ref[:, state:] = (c_total + back_in[0]).astype(gbc_ref.dtype)
    copy_back(1).wait_recv()
    total = sums2[...] + back_in[1]
    inside, x_in = sums1[:, :heads], sums1[:, heads:]
    g_in, both = total[:, :heads], span[:1, heads:] * total[:, heads:]
    dt_all = cols1[0, :, heads:]
    after = (row_at <= col_at).astype(F32)
    before = (row_at > col_at).astype(F32)
    d_log = (
        both
        + exact_dot(before, dt_all * x_in, 1, 0)
        + exact_dot(after, g_in - dt_all * inside, 1, 0)
        + exact_dot(after, row_sums[...], 1, 1)
    )
    dlogit_ref[...] = (inside + x_in - rate * d_log) * jax.nn.sigmoid(logit_ref[...])
    d_rate = -jnp.sum(dt_all * d_log, axis=0, keepdims=True)
    drate_ref[...] = jnp.broadcast_to(
        jnp.concatenate([d_rate, jnp.zeros_like(d_rate)], axis=1), drate_ref.shape
    )
    copy_span().wait_send()
    copy_c().wait_send()
    copy_back(0).wait_send()
    copy_back(1).wait_send()

    def settle(k, unused):
        copy_g(k).wait_send()
        pl.when(jnp.logical_not(last))(lambda: copy_e(k).wait_send())
        pl.when(jnp.logical_not(first))(lambda: copy_f(k).wait_send())
        return unused

    lax.fori_loop(0, chunks, settle, 0)


def weight_kernel(
    n, m, t_ref, g_ref, rate_ref, out_ref, rate_out,
    acc, got, ring, r_acc, r_got, sem, out_sem, r_sem,
):
    chunks, blocks, rows = acc.shape[0], acc.shape[1], acc.shape[2]
    piece = chunks * rows
    seq, dp = lax.axis_index("seq"), lax.axis_index("dp")
    dp_steps, seq_steps, bit = [], [], 1
    while bit < m:
        dp_steps.append(("dp", bit, lax.rem(lax.div(dp, bit), 2)))
        bit *= 2
    bit = 1
    while bit < n:
        seq_steps.append(("seq", bit, lax.rem(lax.div(seq, bit), 2)))
        bit *= 2
    count = len(dp_steps) + len(seq_steps)
    orders = (dp_steps + seq_steps, dp_steps[:1] + seq_steps + dp_steps[1:])

    def peer(c, s):
        axis, bit, mine = orders[c % 2][s]
        return {axis: lax.axis_index(axis) + bit - 2 * bit * mine}

    def dp_peer(k):
        other, bit = dp, 1
        while bit < m:
            if k & bit:
                other = other + bit - 2 * bit * lax.rem(lax.div(dp, bit), 2)
            bit *= 2
        return {"dp": other}

    barrier = pltpu.get_barrier_semaphore()
    friends = [dp_peer(k) for k in range(1, m)] + [
        peer(0, s) for s in range(len(dp_steps), count)
    ]
    for friend in friends:
        pl.semaphore_signal(
            barrier, inc=1, device_id=friend, device_id_type=pl.DeviceIdType.MESH
        )

    starts, offsets = [], []
    for order in orders:
        base, width, total = 0, blocks, 0
        starts.append([])
        for unused, unused, mine in order:
            width //= 2
            starts[-1].append((base + width * mine, base + width * (1 - mine), width))
            base = base + width * mine
            if len(starts) == 1:
                offsets.append(total)
                total += width

    def copy(c, s):
        keep, give, size = starts[c % 2][s]
        return pltpu.make_async_remote_copy(
            src_ref=acc.at[c, pl.ds(give, size)],
            dst_ref=got.at[c, pl.ds(offsets[s], size)],
            send_sem=sem.at[0, c, s], recv_sem=sem.at[1, c, s],
            device_id=peer(c, s), device_id_type=pl.DeviceIdType.MESH,
        )

    def rate_copy(s):
        return pltpu.make_async_remote_copy(
            src_ref=r_acc.at[s], dst_ref=r_got.at[s],
            send_sem=r_sem.at[0, s], recv_sem=r_sem.at[1, s],
            device_id=peer(0, s), device_id_type=pl.DeviceIdType.MESH,
        )

    def out_copy(c, k):
        return pltpu.make_async_remote_copy(
            src_ref=ring.at[0, c], dst_ref=ring.at[k, c],
            send_sem=out_sem.at[0, c, k], recv_sem=out_sem.at[1, c, k],
            device_id=dp_peer(k), device_id_type=pl.DeviceIdType.MESH,
        )

    g = g_ref[...]
    r_acc[0] = rate_ref[...]
    block = 128
    for first in range(0, t_ref.shape[1], block):
        product = dot(t_ref[:, first : first + block], g, 0, 0)
        for part in range(0, block, rows):
            row = first + part
            owner, inner = row // (m * piece), row % (m * piece)
            chunk, place = inner % piece // rows, 0
            for axis, bit, unused in orders[chunk % 2]:
                index = inner // piece if axis == "dp" else owner
                place = 2 * place + index // bit % 2
            acc[chunk, place] = product[part : part + rows]
    pl.semaphore_wait(barrier, len(friends))
    for c in range(chunks):
        copy(c, 0).start()
    rate_copy(0).start()
    for s in range(count):
        for c in range(chunks):
            copy(c, s).wait_recv()
            keep, give, size = starts[c % 2][s]
            value = acc[c, pl.ds(keep, size)] + got[c, pl.ds(offsets[s], size)]
            if s + 1 < count:
                acc[c, pl.ds(keep, size)] = value
                copy(c, s + 1).start()
            else:
                ring[0, c] = value[0]
                for k in range(1, m):
                    out_copy(c, k).start()
        rate_copy(s).wait_recv()
        r_acc[s + 1] = r_acc[s] + r_got[s]
        if s + 1 < count:
            rate_copy(s + 1).start()
    rate_out[...] = r_acc[count]
    for c in range(chunks):
        for k in range(m):
            if k > 0:
                out_copy(c, k).wait_recv()
            where = dp_peer(k)["dp"] if k > 0 else dp
            out_ref[pl.ds(where * piece + c * rows, rows)] = ring[k, c]
    for c in range(chunks):
        for s in range(count):
            copy(c, s).wait_send()
        for k in range(1, m):
            out_copy(c, k).wait_send()
    for s in range(count):
        rate_copy(s).wait_send()


def shards(layer_input, projection, ssm_input, step_logit, decay_rate, output_grad):
    tokens, x_rows, logit, grad_rows = layer_input[0], ssm_input[0], step_logit[0], output_grad[0]
    length, full = x_rows.shape
    heads = logit.shape[1]
    size = full // heads
    state = projection.shape[1] // 2
    groups = heads // HEADS
    width = HEADS * size
    count = lax.axis_size("seq")
    limit = 60 * 2**20
    vmem = pl.BlockSpec(memory_space=pltpu.VMEM)
    slots = pltpu.VMEM((groups, state, width), F32)
    rows_in = pltpu.VMEM((groups, length, width), F32)
    half = pltpu.VMEM((groups, state, width), BF16)
    square = pltpu.VMEM((length, length), F32)
    sums = pltpu.VMEM((length, state), F32)
    short = pltpu.VMEM((length, state), BF16)
    by_lane = pltpu.VMEM((length, 2 * heads), F32)
    cols = pltpu.VMEM((groups, length, 2 * heads), F32)
    strip = pltpu.VMEM((8, 2 * heads), F32)
    two = pltpu.VMEM((2, length, state), F32)
    grad_x, grad_logit, rate_rows, grad_bc = pl.pallas_call(
        functools.partial(layer_kernel, count, size),
        in_specs=[vmem] * 6,
        out_specs=[vmem] * 4,
        out_shape=[
            jax.ShapeDtypeStruct((length, full), BF16),
            jax.ShapeDtypeStruct((length, heads), F32),
            jax.ShapeDtypeStruct((8, 2 * heads), F32),
            jax.ShapeDtypeStruct((length, 2 * state), BF16),
        ],
        scratch_shapes=[short] * 3
        + [cols] * 2
        + [pltpu.VMEM((groups, HEADS, length), F32), strip, strip, sums, sums]
        + [half] * 4
        + [square, square, sums, sums]
        + [by_lane, by_lane, pltpu.VMEM((heads, length), F32), two, two]
        + [rows_in] * 2
        + [slots] * 4
        + [pltpu.SemaphoreType.DMA((2, 4))]
        + [pltpu.SemaphoreType.DMA((2, groups))] * 3,
        compiler_params=pltpu.CompilerParams(
            collective_id=0, has_side_effects=True, vmem_limit_bytes=limit
        ),
        name="layer_gradients",
    )(tokens, projection, x_rows, grad_rows, logit, decay_rate[None, :])
    members = lax.axis_size("dp")
    blocks = count * members
    piece = tokens.shape[1] // blocks
    chunks = max(1, min(8, piece // 8))
    rows = piece // chunks
    levels = blocks.bit_length() - 1
    weight_rows, rate_sum = pl.pallas_call(
        functools.partial(weight_kernel, count, members),
        in_specs=[vmem] * 3,
        out_specs=[vmem] * 2,
        out_shape=[
            jax.ShapeDtypeStruct((members * piece, 2 * state), F32),
            jax.ShapeDtypeStruct((8, 128), F32),
        ],
        scratch_shapes=[
            pltpu.VMEM((chunks, blocks, rows, 2 * state), F32),
            pltpu.VMEM((chunks, blocks, rows, 2 * state), F32),
            pltpu.VMEM((members, chunks, rows, 2 * state), F32),
            pltpu.VMEM((levels + 1, 8, 128), F32),
            pltpu.VMEM((levels, 8, 128), F32),
            pltpu.SemaphoreType.DMA((2, chunks, levels)),
            pltpu.SemaphoreType.DMA((2, chunks, members)),
            pltpu.SemaphoreType.DMA((2, levels)),
        ],
        compiler_params=pltpu.CompilerParams(
            collective_id=1, has_side_effects=True, vmem_limit_bytes=limit
        ),
        name="weight_gradient",
    )(tokens, grad_bc, rate_rows)
    rate_sum = rate_sum[0, :heads]
    return (grad_x[None], grad_logit[None], rate_sum, weight_rows)


def solution(mesh):
    placed = (
        P("dp", "seq", None),
        P(),
        P("dp", "seq", None),
        P("dp", "seq", None),
        P(),
        P("dp", "seq", None),
    )
    return jax.shard_map(
        shards,
        mesh=mesh,
        in_specs=placed,
        out_specs=(P("dp", "seq", None), P("dp", "seq", None), P(), P("seq", None)),
        check_vma=False,
    )
```

time: 130 us -> 124 us (0.954)
  other arithmetic: 4.01 us -> 0 us
  Pallas kernels: 111 us -> 115 us
  local copies, waits for them, and re-layouts: 10.4 us -> 7.36 us
  matrix products: 3.02 us -> 0 us
    dot_general x4 -> x0, matrix products: 3.02 us -> none  [the longest x1 1.23 us: shards(): jnp.dot((position[:, None] <= position[None, :]).astype(F32), change, pre...]
    pallas_call x1, Pallas kernels: 74.4 us -> 77.4 us  [shards(): pl.pallas_call(functools.partial(layer_kernel, count, size), in_specs=[vm...]
    unnamed x16 -> x6, local copies, waits for them, and re-layouts: 3.89 us -> 6.11 us
    concatenate x1 -> x0, local copies, waits for them, and re-layouts: 1.96 us -> none  [shards(): jnp.concatenate([by_group(v) for v in (log_decay, dt, to_end, grow)], axi...]
    pallas_call x1 -> x0, other arithmetic: 1.4 us -> none  [shards(): pl.pallas_call(functools.partial(layer_kernel, count, size), in_specs=[vm...]
where the time goes in v3:
time: 124 us; the launch traced here: 123 us
  Pallas kernels  115 us (93%)
  local copies, waits for them, and re-layouts  7.36 us (6%)
    pallas_call x1, Pallas kernels, shards(): pl.pallas_call(functools.partial(layer_kernel, count, size), in_specs=[vm...  77.4 us
    pallas_call x1, Pallas kernels, shards(): pl.pallas_call(functools.partial(weight_kernel, count, members), in_specs...  38 us
    unnamed x6, local copies, waits for them, and re-layouts  6.11 us

profile of v3, /device:TPU:0, one launch (start us, length us, event | category | flops | bytes accessed | tf_op | source)
XLA Modules:
  0.0 123.4 jit_solution(13358841239806125217)
XLA Ops:
  0.6 1.5 %copy.10 = f32[1,128,64]{2,1,0:T(8,128)} copy(f32[1,128,64]{1,2,0:T(8,128)} %param.9) | data formatting | bytes 65536 | tf_op args[3]
  2.1 77.4 %layer_gradients.1 = (bf16[128,4096]{1,0:T(8,128)(2,1)}, f32[128,64]{1,0:T(8,128)}, f32[8,128]{1,0:T(8,128)}, bf16[128,256]{1,0:T(8,128)(2,1)}) custom-call(bf16[128,4096]{1,0:T(8,128)(2,1)} %bitcast.9, bf16[4096,256]{1,0:T(8,128)(2,1)} %w_ref.1, bf16[128,4096]{1,0:T(8,128)(2,1)} %bitcast.12, bf16[128,4096]{1,0:T(8,128)(2,1)} %bitcast.13, ...), custom_call_target="tpu_custom_call" | custom-call | tf_op jit(solution)/shard_map/layer_gradients/pallas_call | solution.py:454
  79.5 1.5 %copy.11 = f32[1,128,64]{1,2,0:T(8,128)} copy(f32[1,128,64]{2,1,0:T(8,128)} %bitcast.15) | data formatting | bytes 65536
  81.0 38.0 %weight_gradient.1 = (f32[512,256]{1,0:T(8,128)}, f32[8,128]{1,0:T(8,128)}) custom-call(bf16[128,4096]{1,0:T(8,128)(2,1)} %bitcast.10, bf16[128,256]{1,0:T(8,128)(2,1)} %get-tuple-element.12.g_ref, f32[8,128]{1,0:T(8,128)} %get-tuple-element.13.rate_ref), custom_call_target="tpu_custom_call" | custom-call | tf_op jit(solution)/shard_map/weight_gradient/pallas_call | solution.py:485
  119.0 0.0 copy-start
  119.0 1.2 %slice_bitcast_fusion = f32[64]{0:T(128)} fusion(f32[8,128]{1,0:T(8,128)} %get-tuple-element.14), kind=kLoop, calls=%fused_computation | loop fusion | bytes 512 | tf_op jit(solution)/shard_map/squeeze | solution.py:508
  120.3 2.3 %copy.14 = bf16[1,128,4096]{2,1,0:T(8,128)(2,1)} copy(bf16[1,128,4096]{2,1,0:T(8,128)(2,1)} %bitcast.11) | data formatting | bytes 2097152
  122.6 0.0 copy-done
  122.6 0.8 copy.15
Async XLA Ops:
  119.0 3.5 %copy-start = (f32[512,256]{1,0:T(8,128)S(1)}, f32[512,256]{1,0:T(8,128)}, u32[]{:S(2)}) copy-start(f32[512,256]{1,0:T(8,128)} %get-tuple-element.27) | copy-start | bytes 1572868

commit v4 on v3

--- a/solution.py
+++ b/solution.py
@@ -30,18 +30,39 @@
     return jnp.where(lane < size, cols[:, j : j + 1], cols[:, j + 1 : j + 2])
 
 
+def flip(index, bits, limit):
+    other, bit = index, 1
+    while bit < limit:
+        if bits & bit:
+            other = other + bit - 2 * bit * lax.rem(lax.div(index, bit), 2)
+        bit *= 2
+    return other
+
+
+def ordered(n):
+    def key(r):
+        return (r & -r) or n, -r
+
+    return sorted(range(0, n, 2), key=key)
+
+
 def layer_kernel(
-    n, size, t_ref, w_ref, x_ref, g_ref, logit_ref, rate_ref,
-    dx_ref, dlogit_ref, drate_ref, gbc_ref,
+    n, m, size, fused, t_ref, w_ref, x_ref, g_ref, logit_ref, rate_ref,
+    dx_ref, dlogit_ref, drate_ref, weight_ref,
     b_ref, c_ref, c_in, cols1, cols2, rows_ref, span, span_in, cf, cf_in,
     e_own, e_other, f_own, f_other, scores, d_scores, d_b, d_c,
     sums1, sums2, row_sums, back, back_in,
     gs_snd, gs_in, e_in, f_in, e_snd, f_snd,
-    small_sem, gs_sem, e_sem, f_sem,
+    small_sem, gs_sem, e_sem, f_sem, *more,
 ):
+    if fused:
+        (
+            tok_snd, tok_in, tok, gbc_snd, gbc_in, gbc, acc, got, out, rate_dp, rate_got, rate_acc,
+            tok_sem, gbc_sem, acc_sem, out_sem, rate_sem,
+        ) = more
     chunks = gs_snd.shape[0]
     length, state = b_ref.shape
-    heads = logit_ref.shape[1]
+    heads = logit_ref.shape[0]
     width = HEADS * size
     nz = n // 2
     me = lax.axis_index("seq")
@@ -51,19 +72,29 @@
     first, last = z == 0, z == nz - 1
     barrier = pltpu.get_barrier_semaphore()
 
-    def greet(who):
+    def greet(who, axis="seq"):
         pl.semaphore_signal(
-            barrier, inc=1, device_id={"seq": who}, device_id_type=pl.DeviceIdType.MESH
+            barrier, inc=1, device_id={axis: who}, device_id_type=pl.DeviceIdType.MESH
         )
 
     greet(partner)
     pl.when(jnp.logical_not(first))(lambda: greet(me - 2))
     pl.when(jnp.logical_not(last))(lambda: greet(me + 2))
-
-    def send(src, dst, sems, k, who):
+    greeters = 1
+    if fused:
+        bit = 4
+        while bit < n:
+            greet(flip(me, bit, n))
+            greeters += 1
+            bit *= 2
+        for k in range(1, m):
+            greet(flip(lax.axis_index("dp"), k, m), "dp")
+            greeters += 1
+
+    def send(src, dst, sems, k, who, axis="seq"):
         return pltpu.make_async_remote_copy(
             src_ref=src, dst_ref=dst, send_sem=sems.at[0, k], recv_sem=sems.at[1, k],
-            device_id={"seq": who}, device_id_type=pl.DeviceIdType.MESH,
+            device_id={axis: who}, device_id_type=pl.DeviceIdType.MESH,
         )
 
     def copy_span():
@@ -92,7 +123,7 @@
         return pl.ds(pl.multiple_of(k * width, width), width)
 
     logit, rate = logit_ref[...], rate_ref[...]
-    dt_all = jnp.maximum(logit, 0.0) + jnp.log1p(jnp.exp(-jnp.abs(logit)))
+    dt_all = (jnp.maximum(logit, 0.0) + jnp.log1p(jnp.exp(-jnp.abs(logit)))).T
     row_at = lax.broadcasted_iota(jnp.int32, (length, length), 0)
     col_at = lax.broadcasted_iota(jnp.int32, (length, length), 1)
     until = (row_at >= col_at).astype(F32)
@@ -115,8 +146,8 @@
         return unused
 
     end = jnp.logical_or(first, last)
-    pl.when(end)(lambda: pl.semaphore_wait(barrier, min(nz, 2)))
-    pl.when(jnp.logical_not(end))(lambda: pl.semaphore_wait(barrier, 3))
+    pl.when(end)(lambda: pl.semaphore_wait(barrier, min(nz - 1, 1) + greeters))
+    pl.when(jnp.logical_not(end))(lambda: pl.semaphore_wait(barrier, 2 + greeters))
     copy_span().start()
     lax.fori_loop(0, EARLY, scale, 0)
     bc = dot(t_ref[...], w_ref[...], 1, 0).astype(BF16)
@@ -124,16 +155,6 @@
     c_ref[...] = bc[:, state:]
     cf[...] = bc[:, state:].astype(F32)
     copy_c().start()
-    lax.fori_loop(EARLY, chunks, scale, 0)
-
-    @pl.when(first)
-    def _():
-        e_in[...] = jnp.zeros_like(e_in)
-
-    @pl.when(last)
-    def _():
-        f_in[...] = jnp.zeros_like(f_in)
-
     scores[...] = dot(b_ref[...], c_ref[...], 1, 1)
     for ref in (d_scores, d_b, d_c, sums1, sums2, row_sums, back):
         ref[...] = jnp.zeros_like(ref)
@@ -246,11 +267,20 @@
     delay = LAG * lax.max(z, nz - 1 - z)
 
     def step(t, unused):
+        @pl.when(t + EARLY < chunks)
+        def _():
+            scale(t + EARLY, 0)
+
         kf = t - LAG * z
 
         @pl.when(jnp.logical_and(kf >= 0, kf < chunks))
         def _():
             pl.when(jnp.logical_not(first))(lambda: copy_e(kf).wait_recv())
+
+            @pl.when(first)
+            def _():
+                e_in[kf] = jnp.zeros_like(e_in[kf])
+
             forward(kf)
             pl.when(jnp.logical_not(last))(lambda: copy_e(kf).start())
 
@@ -260,21 +290,109 @@
         def _():
             copy_g(kb).wait_recv()
             pl.when(jnp.logical_not(last))(lambda: copy_f(kb).wait_recv())
+
+            @pl.when(last)
+            def _():
+                f_in[kb] = jnp.zeros_like(f_in[kb])
+
             backward(kb)
             pl.when(jnp.logical_not(first))(lambda: copy_f(kb).start())
 
         kg = t - delay
         pl.when(jnp.logical_and(kg >= 0, kg < chunks))(lambda: gradients(kg))
         return unused
+
+    if fused:
+        dp = lax.axis_index("dp")
+        piece = tok.shape[1]
+
+        def columns(s, k):
+            first_column = (s * m + flip(dp, k, m)) * piece
+            return t_ref[:, pl.ds(pl.multiple_of(first_column, piece), piece)].astype(F32)
+
+        def copy_tokens(k):
+            return send(
+                tok_snd.at[k - 1], tok_in.at[k - 1], tok_sem, k - 1, flip(dp, k, m), "dp"
+            )
+
+        def copy_gbc(i, k):
+            return send(
+                gbc_snd.at[i], gbc_in.at[k - 1, i], gbc_sem, (m - 1) * i + k - 1,
+                flip(dp, k, m), "dp",
+            )
+
+        def copy_acc(i, r):
+            bit = r & -r
+            return send(
+                acc.at[i, r], got.at[i, r - 1], acc_sem, (n - 1) * i + r - 1, flip(me, bit, n)
+            )
+
+        def copy_out(i, k):
+            return send(
+                out.at[i, 0], out.at[i, k], out_sem, m * i + k, flip(dp, k, m), "dp"
+            )
+
+        def copy_rate_dp(k):
+            return send(
+                rate_dp.at[0], rate_dp.at[k], rate_sem, k - 1, flip(dp, k, m), "dp"
+            )
+
+        def copy_rate(i):
+            return send(
+                rate_acc.at[i], rate_got.at[i], rate_sem, m - 1 + i, flip(me, 1 << i, n)
+            )
+
+        def spread(s, unused):
+            for k in range(1, m):
+                tok_snd[k - 1, s] = columns(s, k)
+            return unused
+
+        lax.fori_loop(0, n, spread, 0)
+        for k in range(1, m):
+            copy_tokens(k).start()
 
     lax.fori_loop(0, chunks + delay, step, 0)
     copy_back(0).start()
     copy_back(1).start()
     dk = d_scores[...].astype(BF16)
-    gbc_ref[:, :state] = (d_b[...] + dot(dk, c_ref[...], 1, 0)).astype(gbc_ref.dtype)
+    grad_b = (d_b[...] + dot(dk, c_ref[...], 1, 0)).astype(BF16)
+    if fused:
+        gbc_snd[0] = grad_b.astype(F32)
+        for k in range(1, m):
+            copy_gbc(0, k).start()
+        gbc[0, :length] = grad_b
+    else:
+        weight_ref[:, :state] = grad_b
     c_total = d_c[...] + dot(dk, b_ref[...], 0, 0)
     copy_back(0).wait_recv()
-    gbc_ref[:, state:] = (c_total + back_in[0]).astype(gbc_ref.dtype)
+    grad_c = (c_total + back_in[0]).astype(BF16)
+    if fused:
+        gbc_snd[1] = grad_c.astype(F32)
+        for k in range(1, m):
+            copy_gbc(1, k).start()
+        gbc[1, :length] = grad_c
+        for k in range(1, m):
+            copy_tokens(k).wait_recv()
+
+        def place_tokens(r, unused):
+            s = r
+            for k in range(m):
+                block = columns(s, k) if k == 0 else tok_in[k - 1, s]
+                tok[s, :, k * length : (k + 1) * length] = block.T.astype(BF16)
+            return unused
+
+        lax.fori_loop(0, n, place_tokens, 0)
+        order = ordered(n)
+        for i in range(2):
+            for k in range(1, m):
+                copy_gbc(i, k).wait_recv()
+                gbc[i, k * length : (k + 1) * length] = gbc_in[k - 1, i].astype(BF16)
+            for r in [r + 1 for r in order] + order:
+                acc[i, r] = dot(tok[flip(me, r, n)], gbc[i], 1, 0)
+                if r % 2:
+                    copy_acc(i, r).start()
+    else:
+        weight_ref[:, state:] = grad_c
     copy_back(1).wait_recv()
     total = sums2[...] + back_in[1]
     inside, x_in = sums1[:, :heads], sums1[:, heads:]
@@ -288,11 +406,64 @@
         + exact_dot(after, g_in - dt_all * inside, 1, 0)
         + exact_dot(after, row_sums[...], 1, 1)
     )
-    dlogit_ref[...] = (inside + x_in - rate * d_log) * jax.nn.sigmoid(logit_ref[...])
     d_rate = -jnp.sum(dt_all * d_log, axis=0, keepdims=True)
-    drate_ref[...] = jnp.broadcast_to(
-        jnp.concatenate([d_rate, jnp.zeros_like(d_rate)], axis=1), drate_ref.shape
+    d_rate = jnp.broadcast_to(
+        jnp.concatenate([d_rate, jnp.zeros_like(d_rate)], axis=1), (8, 2 * heads)
     )
+    if fused:
+        rate_dp[0] = d_rate
+        for k in range(1, m):
+            copy_rate_dp(k).start()
+    else:
+        drate_ref[...] = d_rate
+    d_step = inside + x_in - rate_ref[...] * d_log
+    dlogit_ref[...] = d_step.T * jax.nn.sigmoid(logit_ref[...])
+    if fused:
+        for i in range(2):
+            for r in order:
+                bit = 1
+                while bit < ((r & -r) or n):
+                    copy_acc(i, r + bit).wait_recv()
+                    acc[i, r] += got[i, r + bit - 1]
+                    bit *= 2
+                if r:
+                    copy_acc(i, r).start()
+            out[i, 0] = acc[i, 0]
+            for k in range(1, m):
+                copy_out(i, k).start()
+            if i == 0:
+                parts = [rate_dp[0]]
+                for k in range(1, m):
+                    copy_rate_dp(k).wait_recv()
+                    parts.append(rate_dp[k])
+                while len(parts) > 1:
+                    parts = [p + q for p, q in zip(parts[::2], parts[1::2])]
+                rate_acc[0] = parts[0]
+                copy_rate(0).start()
+        stages = n.bit_length() - 1
+        for i in range(stages):
+            copy_rate(i).wait_recv()
+            rate_acc[i + 1] = rate_acc[i] + rate_got[i]
+            if i + 1 < stages:
+                copy_rate(i + 1).start()
+        drate_ref[...] = rate_acc[stages, :1, :heads]
+        for i in range(2):
+            for k in range(m):
+                if k:
+                    copy_out(i, k).wait_recv()
+                first_row = pl.multiple_of(flip(dp, k, m) * piece, piece)
+                weight_ref[pl.ds(first_row, piece), i * state : (i + 1) * state] = out[i, k]
+        for k in range(1, m):
+            copy_tokens(k).wait_send()
+            copy_rate_dp(k).wait_send()
+            for i in range(2):
+                copy_gbc(i, k).wait_send()
+                copy_out(i, k).wait_send()
+        for i in range(2):
+            for r in range(1, n):
+                copy_acc(i, r).wait_send()
+        for i in range(stages):
+            copy_rate(i).wait_send()
     copy_span().wait_send()
     copy_c().wait_send()
     copy_back(0).wait_send()
@@ -451,17 +622,13 @@
     cols = pltpu.VMEM((groups, length, 2 * heads), F32)
     strip = pltpu.VMEM((8, 2 * heads), F32)
     two = pltpu.VMEM((2, length, state), F32)
-    grad_x, grad_logit, rate_rows, grad_bc = pl.pallas_call(
-        functools.partial(layer_kernel, count, size),
-        in_specs=[vmem] * 6,
-        out_specs=[vmem] * 4,
-        out_shape=[
-            jax.ShapeDtypeStruct((length, full), BF16),
-            jax.ShapeDtypeStruct((length, heads), F32),
-            jax.ShapeDtypeStruct((8, 2 * heads), F32),
-            jax.ShapeDtypeStruct((length, 2 * state), BF16),
-        ],
-        scratch_shapes=[short] * 3
+    members = lax.axis_size("dp")
+    blocks = count * members
+    piece = tokens.shape[1] // blocks
+    levels = blocks.bit_length() - 1
+    fused = piece % 128 == 0
+    scratch = (
+        [short] * 3
         + [cols] * 2
         + [pltpu.VMEM((groups, HEADS, length), F32), strip, strip, sums, sums]
         + [half] * 4
@@ -470,18 +637,53 @@
         + [rows_in] * 2
         + [slots] * 4
         + [pltpu.SemaphoreType.DMA((2, 4))]
-        + [pltpu.SemaphoreType.DMA((2, groups))] * 3,
+        + [pltpu.SemaphoreType.DMA((2, groups))] * 3
+    )
+    rate_shape = jax.ShapeDtypeStruct((8, 2 * heads), F32)
+    weight_shape = jax.ShapeDtypeStruct((length, 2 * state), BF16)
+    if fused:
+        stages = count.bit_length() - 1
+        others = members - 1
+        scratch += [pltpu.VMEM((others, count, length, piece), F32)] * 2
+        scratch += [
+            pltpu.VMEM((count, piece, members * length), BF16),
+            pltpu.VMEM((2, length, state), F32),
+            pltpu.VMEM((others, 2, length, state), F32),
+            pltpu.VMEM((2, members * length, state), BF16),
+            pltpu.VMEM((2, count, piece, state), F32),
+            pltpu.VMEM((2, count - 1, piece, state), F32),
+            pltpu.VMEM((2, members, piece, state), F32),
+            pltpu.VMEM((members, 8, 2 * heads), F32),
+            pltpu.VMEM((stages, 8, 2 * heads), F32),
+            pltpu.VMEM((stages + 1, 8, 2 * heads), F32),
+            pltpu.SemaphoreType.DMA((2, others)),
+            pltpu.SemaphoreType.DMA((2, 2 * others)),
+            pltpu.SemaphoreType.DMA((2, 2 * (count - 1))),
+            pltpu.SemaphoreType.DMA((2, 2 * members)),
+            pltpu.SemaphoreType.DMA((2, others + stages)),
+        ]
+        rate_shape = jax.ShapeDtypeStruct((1, heads), F32)
+        weight_shape = jax.ShapeDtypeStruct((members * piece, 2 * state), F32)
+    grad_x, grad_logit, rate_rows, weights = pl.pallas_call(
+        functools.partial(layer_kernel, count, members, size, fused),
+        in_specs=[vmem] * 6,
+        out_specs=[vmem] * 4,
+        out_shape=[
+            jax.ShapeDtypeStruct((length, full), BF16),
+            jax.ShapeDtypeStruct((heads, length), F32),
+            rate_shape,
+            weight_shape,
+        ],
+        scratch_shapes=scratch,
         compiler_params=pltpu.CompilerParams(
             collective_id=0, has_side_effects=True, vmem_limit_bytes=limit
         ),
         name="layer_gradients",
-    )(tokens, projection, x_rows, grad_rows, logit, decay_rate[None, :])
-    members = lax.axis_size("dp")
-    blocks = count * members
-    piece = tokens.shape[1] // blocks
+    )(tokens, projection, x_rows, grad_rows, logit.T, decay_rate[None, :])
+    if fused:
+        return (grad_x[None], grad_logit.T[None], rate_rows[0], weights)
     chunks = max(1, min(8, piece // 8))
     rows = piece // chunks
-    levels = blocks.bit_length() - 1
     weight_rows, rate_sum = pl.pallas_call(
         functools.partial(weight_kernel, count, members),
         in_specs=[vmem] * 3,
@@ -504,9 +706,9 @@
             collective_id=1, has_side_effects=True, vmem_limit_bytes=limit
         ),
         name="weight_gradient",
-    )(tokens, grad_bc, rate_rows)
+    )(tokens, weights, rate_rows)
     rate_sum = rate_sum[0, :heads]
-    return (grad_x[None], grad_logit[None], rate_sum, weight_rows)
+    return (grad_x[None], grad_logit.T[None], rate_sum, weight_rows)
 
 
 def solution(mesh):

time: 124 us -> 110 us (0.89)
  Pallas kernels: 115 us -> 105 us
  local copies, waits for them, and re-layouts: 7.36 us -> 4.28 us
    pallas_call x2 -> x1, Pallas kernels: 115 us -> 105 us  [shards(): pl.pallas_call(functools.partial(layer_kernel, count, members, size, fuse...]
    unnamed x6 -> x10, local copies, waits for them, and re-layouts: 6.11 us -> 4.28 us
    squeeze x1 -> x0, local copies, waits for them, and re-layouts: 1.25 us -> none  [shards(): rate_sum = rate_sum[0, :heads]]
where the time goes in v4:
time: 110 us
  Pallas kernels  105 us (95%)
  local copies, waits for them, and re-layouts  4.28 us (4%)
    pallas_call x1, Pallas kernels, shards(): pl.pallas_call(functools.partial(layer_kernel, count, members, size, fuse...  105 us
    unnamed x10, local copies, waits for them, and re-layouts  4.28 us

profile of v4, /device:TPU:0, one launch (start us, length us, event | category | flops | bytes accessed | tf_op | source)
XLA Modules:
  0.0 109.7 jit_solution(4517418429506650818)
XLA Ops:
  0.6 104.8 %layer_gradients.1 = (bf16[128,4096]{1,0:T(8,128)(2,1)}, f32[64,128]{1,0:T(8,128)}, f32[1,64]{1,0:T(1,128)}, f32[512,256]{1,0:T(8,128)}) custom-call(bf16[128,4096]{1,0:T(8,128)(2,1)} %bitcast.13, bf16[4096,256]{1,0:T(8,128)(2,1)} %w_ref.1, bf16[128,4096]{1,0:T(8,128)(2,1)} %bitcast.14, bf16[128,4096]{1,0:T(8,128)(2,1)} %bitcast.15, f32[64,128]{1,0:T(8,128)} %bitcast.16, ...), custom_call_target="tpu_custom_call" | custom-call | tf_op jit(solution)/shard_map/layer_gradients/pallas_call | solution.py:667
  105.4 0.0 copy-start.1
  105.4 0.0 copy-start.2
  105.4 0.0 copy-start
  105.5 2.3 %copy.14 = bf16[1,128,4096]{2,1,0:T(8,128)(2,1)} copy(bf16[1,128,4096]{2,1,0:T(8,128)(2,1)} %bitcast.12) | data formatting | bytes 2097152
  107.8 0.0 copy-done.1
  107.8 0.6 copy.15
  108.4 0.0 copy-done.2
  108.4 0.5 copy.16
  108.9 0.0 copy-done
  108.9 0.8 copy.17
Async XLA Ops:
  105.4 2.4 %copy-start.1 = (f32[64,128]{1,0:T(8,128)S(1)}, f32[64,128]{1,0:T(8,128)}, u32[]{:S(2)}) copy-start(f32[64,128]{1,0:T(8,128)} %get-tuple-element.9) | copy-start | bytes 98308
  105.4 3.0 %copy-start.2 = (f32[1,64]{1,0:T(1,128)S(1)}, f32[1,64]{1,0:T(1,128)}, u32[]{:S(2)}) copy-start(f32[1,64]{1,0:T(1,128)} %get-tuple-element.10) | copy-start | bytes 772
  105.4 3.5 %copy-start = (f32[512,256]{1,0:T(8,128)S(1)}, f32[512,256]{1,0:T(8,128)}, u32[]{:S(2)}) copy-start(f32[512,256]{1,0:T(8,128)} %get-tuple-element.19) | copy-start | bytes 1572868

commit v5 on v4

--- a/solution.py
+++ b/solution.py
@@ -47,13 +47,13 @@
 
 
 def layer_kernel(
-    n, m, size, fused, t_ref, w_ref, x_ref, g_ref, logit_ref, rate_ref,
-    dx_ref, dlogit_ref, drate_ref, weight_ref,
+    n, m, size, fused, t_hbm, w_hbm, x_hbm, g_hbm, logit_ref, rate_ref,
+    dx_ref, dlogit_ref, drate_ref, weight_ref, t_ref, w_ref, x_ref, g_ref,
     b_ref, c_ref, c_in, cols1, cols2, rows_ref, span, span_in, cf, cf_in,
     e_own, e_other, f_own, f_other, scores, d_scores, d_b, d_c,
     sums1, sums2, row_sums, back, back_in,
     gs_snd, gs_in, e_in, f_in, e_snd, f_snd,
-    small_sem, gs_sem, e_sem, f_sem, *more,
+    load_sem, small_sem, gs_sem, e_sem, f_sem, *more,
 ):
     if fused:
         (
@@ -71,12 +71,21 @@
     partner = me + 1 - 2 * odd
     first, last = z == 0, z == nz - 1
     barrier = pltpu.get_barrier_semaphore()
+    operands = ((g_hbm, g_ref), (t_hbm, t_ref), (w_hbm, w_ref), (x_hbm, x_ref))
+    load_g, load_t, load_w, load_x = (
+        pltpu.make_async_copy(source, target, load_sem.at[i])
+        for i, (source, target) in enumerate(operands)
+    )
 
     def greet(who, axis="seq"):
         pl.semaphore_signal(
             barrier, inc=1, device_id={axis: who}, device_id_type=pl.DeviceIdType.MESH
         )
 
+    load_g.start()
+    load_t.start()
+    load_w.start()
+    load_x.start()
     greet(partner)
     pl.when(jnp.logical_not(first))(lambda: greet(me - 2))
     pl.when(jnp.logical_not(last))(lambda: greet(me + 2))
@@ -133,10 +142,6 @@
     q1 = jnp.concatenate([log_decay, dt_all], axis=1)
     q2 = jnp.concatenate([to_end, grow_all], axis=1)
     span[...] = jnp.broadcast_to(q2[length - 1 : length, :], span.shape)
-    by_head = q1.T
-    for k in range(chunks):
-        rows_ref[k] = by_head[HEADS * k : HEADS * (k + 1), :]
-
     def scale(k, unused):
         cols1[k] = turn(q1, k)
         cols = turn(q2, k)
@@ -145,16 +150,23 @@
         copy_g(k).start()
         return unused
 
+    load_g.wait()
     end = jnp.logical_or(first, last)
     pl.when(end)(lambda: pl.semaphore_wait(barrier, min(nz - 1, 1) + greeters))
     pl.when(jnp.logical_not(end))(lambda: pl.semaphore_wait(barrier, 2 + greeters))
     copy_span().start()
     lax.fori_loop(0, EARLY, scale, 0)
+    load_t.wait()
+    load_w.wait()
     bc = dot(t_ref[...], w_ref[...], 1, 0).astype(BF16)
     b_ref[...] = bc[:, :state]
     c_ref[...] = bc[:, state:]
     cf[...] = bc[:, state:].astype(F32)
     copy_c().start()
+    by_head = q1.T
+    for k in range(chunks):
+        rows_ref[k] = by_head[HEADS * k : HEADS * (k + 1), :]
+    load_x.wait()
     scores[...] = dot(b_ref[...], c_ref[...], 1, 1)
     for ref in (d_scores, d_b, d_c, sums1, sums2, row_sums, back):
         ref[...] = jnp.zeros_like(ref)
@@ -610,7 +622,8 @@
     groups = heads // HEADS
     width = HEADS * size
     count = lax.axis_size("seq")
-    limit = 60 * 2**20
+    limit = 46 * 2**20
+    away = pl.BlockSpec(memory_space=pltpu.HBM)
     vmem = pl.BlockSpec(memory_space=pltpu.VMEM)
     slots = pltpu.VMEM((groups, state, width), F32)
     rows_in = pltpu.VMEM((groups, length, width), F32)
@@ -627,8 +640,10 @@
     piece = tokens.shape[1] // blocks
     levels = blocks.bit_length() - 1
     fused = piece % 128 == 0
+    rows = pltpu.VMEM((length, full), BF16)
     scratch = (
-        [short] * 3
+        [rows, pltpu.VMEM(projection.shape, BF16), rows, rows]
+        + [short] * 3
         + [cols] * 2
         + [pltpu.VMEM((groups, HEADS, length), F32), strip, strip, sums, sums]
         + [half] * 4
@@ -636,7 +651,7 @@
         + [by_lane, by_lane, pltpu.VMEM((heads, length), F32), two, two]
         + [rows_in] * 2
         + [slots] * 4
-        + [pltpu.SemaphoreType.DMA((2, 4))]
+        + [pltpu.SemaphoreType.DMA((4,)), pltpu.SemaphoreType.DMA((2, 4))]
         + [pltpu.SemaphoreType.DMA((2, groups))] * 3
     )
     rate_shape = jax.ShapeDtypeStruct((8, 2 * heads), F32)
@@ -663,14 +678,14 @@
             pltpu.SemaphoreType.DMA((2, others + stages)),
         ]
         rate_shape = jax.ShapeDtypeStruct((1, heads), F32)
-        weight_shape = jax.ShapeDtypeStruct((members * piece, 2 * state), F32)
+        weight_shape = pltpu.VMEM((members * piece, 2 * state), F32)
     grad_x, grad_logit, rate_rows, weights = pl.pallas_call(
         functools.partial(layer_kernel, count, members, size, fused),
-        in_specs=[vmem] * 6,
+        in_specs=[away] * 4 + [vmem] * 2,
         out_specs=[vmem] * 4,
         out_shape=[
-            jax.ShapeDtypeStruct((length, full), BF16),
-            jax.ShapeDtypeStruct((heads, length), F32),
+            rows,
+            pltpu.VMEM((heads, length), F32),
             rate_shape,
             weight_shape,
         ],
@@ -679,7 +694,10 @@
             collective_id=0, has_side_effects=True, vmem_limit_bytes=limit
         ),
         name="layer_gradients",
-    )(tokens, projection, x_rows, grad_rows, logit.T, decay_rate[None, :])
+    )(
+        *(pltpu.with_memory_space_constraint(v, pltpu.HBM) for v in (tokens, projection, x_rows, grad_rows)),
+        logit.T, decay_rate[None, :],
+    )
     if fused:
         return (grad_x[None], grad_logit.T[None], rate_rows[0], weights)
     chunks = max(1, min(8, piece // 8))

time: 110 us -> 106 us (0.964)
  Pallas kernels: 105 us -> 101 us
    pallas_call x1, Pallas kernels: 105 us -> 101 us  [shards(): pl.pallas_call(functools.partial(layer_kernel, count, members, size, fuse...]
    unnamed x10 -> x8, local copies, waits for them, and re-layouts: 4.28 us -> 4.3 us
where the time goes in v5:
time: 106 us
  Pallas kernels  101 us (95%)
  local copies, waits for them, and re-layouts  4.3 us (4%)
    pallas_call x1, Pallas kernels, shards(): pl.pallas_call(functools.partial(layer_kernel, count, members, size, fuse...  101 us
    unnamed x8, local copies, waits for them, and re-layouts  4.3 us

profile of v5, /device:TPU:0, one launch (start us, length us, event | category | flops | bytes accessed | tf_op | source)
XLA Modules:
  0.0 105.8 jit_solution(96816318360456408)
XLA Ops:
  0.6 0.0 copy-start
  0.6 0.7 copy-done
  1.4 0.0 copy-start.1
  1.4 0.7 copy-done.1
  2.0 100.8 %layer_gradients.1 = (bf16[128,4096]{1,0:T(8,128)(2,1)S(1)}, f32[64,128]{1,0:T(8,128)S(1)}, f32[1,64]{1,0:T(1,128)S(1)}, f32[512,256]{1,0:T(8,128)S(1)}) custom-call(bf16[128,4096]{1,0:T(8,128)(2,1)} %bitcast.17, bf16[4096,256]{1,0:T(8,128)(2,1)} %w_hbm.1, bf16[128,4096]{1,0:T(8,128)(2,1)} %bitcast.18, bf16[128,4096]{1,0:T(8,128)(2,1)} %bitcast.19, ...), custom_call_target="tpu_custom_call" | custom-call | tf_op jit(solution)/shard_map/layer_gradients/pallas_call | solution.py:682
  102.9 1.0 copy.14
  103.8 0.6 copy.15
  104.5 0.8 copy.16
  105.2 0.5 copy.17
Async XLA Ops:
  0.6 0.8 copy-start
  1.4 0.7 copy-start.1

commit v6 on v5

--- a/solution.py
+++ b/solution.py
@@ -12,6 +12,7 @@
 HEADS = 2
 LAG = 3
 EARLY = 3
+PARTS = 1
 
 
 def dot(a, b, ca, cb):
@@ -39,16 +40,9 @@
     return other
 
 
-def ordered(n):
-    def key(r):
-        return (r & -r) or n, -r
-
-    return sorted(range(0, n, 2), key=key)
-
-
 def layer_kernel(
-    n, m, size, fused, t_hbm, w_hbm, x_hbm, g_hbm, logit_ref, rate_ref,
-    dx_ref, dlogit_ref, drate_ref, weight_ref, t_ref, w_ref, x_ref, g_ref,
+    n, m, size, fused, t_hbm, w_hbm, x_hbm, g_hbm, logit_hbm, rate_hbm,
+    dx_ref, dlogit_ref, drate_ref, weight_ref, t_ref, w_ref, x_ref, g_ref, logit_ref, rate_ref,
     b_ref, c_ref, c_in, cols1, cols2, rows_ref, span, span_in, cf, cf_in,
     e_own, e_other, f_own, f_other, scores, d_scores, d_b, d_c,
     sums1, sums2, row_sums, back, back_in,
@@ -71,8 +65,11 @@
     partner = me + 1 - 2 * odd
     first, last = z == 0, z == nz - 1
     barrier = pltpu.get_barrier_semaphore()
-    operands = ((g_hbm, g_ref), (t_hbm, t_ref), (w_hbm, w_ref), (x_hbm, x_ref))
-    load_g, load_t, load_w, load_x = (
+    operands = (
+        (logit_hbm, logit_ref), (rate_hbm, rate_ref),
+        (g_hbm, g_ref), (t_hbm, t_ref), (w_hbm, w_ref), (x_hbm, x_ref),
+    )
+    load_logit, load_rate, load_g, load_t, load_w, load_x = (
         pltpu.make_async_copy(source, target, load_sem.at[i])
         for i, (source, target) in enumerate(operands)
     )
@@ -82,6 +79,8 @@
             barrier, inc=1, device_id={axis: who}, device_id_type=pl.DeviceIdType.MESH
         )
 
+    load_logit.start()
+    load_rate.start()
     load_g.start()
     load_t.start()
     load_w.start()
@@ -91,11 +90,9 @@
     pl.when(jnp.logical_not(last))(lambda: greet(me + 2))
     greeters = 1
     if fused:
-        bit = 4
-        while bit < n:
-            greet(flip(me, bit, n))
+        for r in range(4, n, 2):
+            greet(flip(me, r, n))
             greeters += 1
-            bit *= 2
         for k in range(1, m):
             greet(flip(lax.axis_index("dp"), k, m), "dp")
             greeters += 1
@@ -118,11 +115,15 @@
     def copy_g(k):
         return send(gs_snd.at[k], gs_in.at[k], gs_sem, k, partner)
 
-    def copy_e(k):
-        return send(e_snd.at[k], e_in.at[k], e_sem, k, me + 2)
-
-    def copy_f(k):
-        return send(f_snd.at[k], f_in.at[k], f_sem, k, me - 2)
+    part = state // PARTS
+
+    def copy_e(k, i):
+        rows = pl.ds(i * part, part)
+        return send(e_snd.at[k, rows], e_in.at[k, rows], e_sem, PARTS * k + i, me + 2)
+
+    def copy_f(k, i):
+        rows = pl.ds(i * part, part)
+        return send(f_snd.at[k, rows], f_in.at[k, rows], f_sem, PARTS * k + i, me - 2)
 
     def turn(value, k):
         lanes = value.shape[1]
@@ -131,6 +132,8 @@
     def wide(k):
         return pl.ds(pl.multiple_of(k * width, width), width)
 
+    load_logit.wait()
+    load_rate.wait()
     logit, rate = logit_ref[...], rate_ref[...]
     dt_all = (jnp.maximum(logit, 0.0) + jnp.log1p(jnp.exp(-jnp.abs(logit)))).T
     row_at = lax.broadcasted_iota(jnp.int32, (length, length), 0)
@@ -178,44 +181,65 @@
         return pair_columns(turn(ref[...], k)[:1, :], heads, size)
 
     def forward(k):
-        value = e_in[k]
         weight = pair_columns(cols1[k], heads, size) * pair_columns(cols2[k], 0, size)
         near = dot(b_ref[...], (x_ref[:, wide(k)].astype(F32) * weight).astype(BF16), 0, 0)
         mine, theirs = spans(span, k), spans(span_in, k)
 
-        @pl.when(odd == 0)
+        @pl.when(first)
         def _():
-            e_own[k] = value.astype(BF16)
-            middle = mine * value + near
-            e_other[k] = middle.astype(BF16)
-            e_snd[k] = theirs * middle
-
-        @pl.when(odd == 1)
-        def _():
-            e_other[k] = value.astype(BF16)
-            middle = theirs * value
-            e_own[k] = middle.astype(BF16)
-            e_snd[k] = mine * middle + near
+            e_in[k] = jnp.zeros_like(e_in[k])
+
+        for i in range(PARTS):
+            rows = slice(i * part, (i + 1) * part)
+            pl.when(jnp.logical_not(first))(lambda: copy_e(k, i).wait_recv())
+            value = e_in[k, rows]
+
+            @pl.when(odd == 0)
+            def _():
+                e_own[k, rows] = value.astype(BF16)
+                middle = mine * value + near[rows]
+                e_other[k, rows] = middle.astype(BF16)
+                e_snd[k, rows] = theirs * middle
+
+            @pl.when(odd == 1)
+            def _():
+                e_other[k, rows] = value.astype(BF16)
+                middle = theirs * value
+                e_own[k, rows] = middle.astype(BF16)
+                e_snd[k, rows] = mine * middle + near[rows]
+
+            pl.when(jnp.logical_not(last))(lambda: copy_e(k, i).start())
 
     def backward(k):
-        value = f_in[k]
+        copy_g(k).wait_recv()
         near = dot(c_ref[...], gs_snd[k].astype(BF16), 0, 0)
         far = dot(c_in[...], gs_in[k].astype(BF16), 0, 0)
         mine, theirs = spans(span, k), spans(span_in, k)
 
-        @pl.when(odd == 0)
+        @pl.when(last)
         def _():
-            f_other[k] = value.astype(BF16)
-            middle = theirs * value + far
-            f_own[k] = middle.astype(BF16)
-            f_snd[k] = mine * middle + near
-
-        @pl.when(odd == 1)
-        def _():
-            f_own[k] = value.astype(BF16)
-            middle = mine * value + near
-            f_other[k] = middle.astype(BF16)
-            f_snd[k] = theirs * middle + far
+            f_in[k] = jnp.zeros_like(f_in[k])
+
+        for i in range(PARTS):
+            rows = slice(i * part, (i + 1) * part)
+            pl.when(jnp.logical_not(last))(lambda: copy_f(k, i).wait_recv())
+            value = f_in[k, rows]
+
+            @pl.when(odd == 0)
+            def _():
+                f_other[k, rows] = value.astype(BF16)
+                middle = theirs * value + far[rows]
+                f_own[k, rows] = middle.astype(BF16)
+                f_snd[k, rows] = mine * middle + near[rows]
+
+            @pl.when(odd == 1)
+            def _():
+                f_own[k, rows] = value.astype(BF16)
+                middle = mine * value + near[rows]
+                f_other[k, rows] = middle.astype(BF16)
+                f_snd[k, rows] = theirs * middle + far[rows]
+
+            pl.when(jnp.logical_not(first))(lambda: copy_f(k, i).start())
 
     def gradients(k):
         cols, rows = cols1[k], rows_ref[k]
@@ -285,31 +309,9 @@
 
         kf = t - LAG * z
 
-        @pl.when(jnp.logical_and(kf >= 0, kf < chunks))
-        def _():
-            pl.when(jnp.logical_not(first))(lambda: copy_e(kf).wait_recv())
-
-            @pl.when(first)
-            def _():
-                e_in[kf] = jnp.zeros_like(e_in[kf])
-
-            forward(kf)
-            pl.when(jnp.logical_not(last))(lambda: copy_e(kf).start())
-
+        pl.when(jnp.logical_and(kf >= 0, kf < chunks))(lambda: forward(kf))
         kb = t - LAG * (nz - 1 - z)
-
-        @pl.when(jnp.logical_and(kb >= 0, kb < chunks))
-        def _():
-            copy_g(kb).wait_recv()
-            pl.when(jnp.logical_not(last))(lambda: copy_f(kb).wait_recv())
-
-            @pl.when(last)
-            def _():
-                f_in[kb] = jnp.zeros_like(f_in[kb])
-
-            backward(kb)
-            pl.when(jnp.logical_not(first))(lambda: copy_f(kb).start())
-
+        pl.when(jnp.logical_and(kb >= 0, kb < chunks))(lambda: backward(kb))
         kg = t - delay
         pl.when(jnp.logical_and(kg >= 0, kg < chunks))(lambda: gradients(kg))
         return unused
@@ -334,10 +336,8 @@
             )
 
         def copy_acc(i, r):
-            bit = r & -r
-            return send(
-                acc.at[i, r], got.at[i, r - 1], acc_sem, (n - 1) * i + r - 1, flip(me, bit, n)
-            )
+            who = partner if r % 2 else flip(me, r, n)
+            return send(acc.at[i, r], got.at[i, r - 1], acc_sem, (n - 1) * i + r - 1, who)
 
         def copy_out(i, k):
             return send(
@@ -349,10 +349,16 @@
                 rate_dp.at[0], rate_dp.at[k], rate_sem, k - 1, flip(dp, k, m), "dp"
             )
 
-        def copy_rate(i):
-            return send(
-                rate_acc.at[i], rate_got.at[i], rate_sem, m - 1 + i, flip(me, 1 << i, n)
-            )
+        def copy_rate_x():
+            return send(rate_acc.at[0], rate_got.at[0], rate_sem, m - 1, partner)
+
+        def copy_rate_z(j):
+            return send(rate_acc.at[1], rate_got.at[j], rate_sem, m - 1 + j, flip(me, 2 * j, n))
+
+        def tree(parts):
+            while len(parts) > 1:
+                parts = [p + q for p, q in zip(parts[::2], parts[1::2])]
+            return parts[0]
 
         def spread(s, unused):
             for k in range(1, m):
@@ -394,7 +400,7 @@
             return unused
 
         lax.fori_loop(0, n, place_tokens, 0)
-        order = ordered(n)
+        order = list(range(n - 2, -1, -2))
         for i in range(2):
             for k in range(1, m):
                 copy_gbc(i, k).wait_recv()
@@ -431,34 +437,41 @@
     d_step = inside + x_in - rate_ref[...] * d_log
     dlogit_ref[...] = d_step.T * jax.nn.sigmoid(logit_ref[...])
     if fused:
-        for i in range(2):
-            for r in order:
-                bit = 1
-                while bit < ((r & -r) or n):
-                    copy_acc(i, r + bit).wait_recv()
-                    acc[i, r] += got[i, r + bit - 1]
-                    bit *= 2
-                if r:
-                    copy_acc(i, r).start()
-            out[i, 0] = acc[i, 0]
+
+        def join(i, r):
+            copy_acc(i, r + 1).wait_recv()
+            acc[i, r] += got[i, r]
+            if r:
+                copy_acc(i, r).start()
+
+        def finish(i):
+            value = acc[i, 0]
+            for r in order[:-1]:
+                copy_acc(i, r).wait_recv()
+                value += got[i, r - 1]
+            out[i, 0] = value
             for k in range(1, m):
                 copy_out(i, k).start()
-            if i == 0:
-                parts = [rate_dp[0]]
-                for k in range(1, m):
-                    copy_rate_dp(k).wait_recv()
-                    parts.append(rate_dp[k])
-                while len(parts) > 1:
-                    parts = [p + q for p, q in zip(parts[::2], parts[1::2])]
-                rate_acc[0] = parts[0]
-                copy_rate(0).start()
-        stages = n.bit_length() - 1
-        for i in range(stages):
-            copy_rate(i).wait_recv()
-            rate_acc[i + 1] = rate_acc[i] + rate_got[i]
-            if i + 1 < stages:
-                copy_rate(i + 1).start()
-        drate_ref[...] = rate_acc[stages, :1, :heads]
+
+        for r in order:
+            join(0, r)
+        for k in range(1, m):
+            copy_rate_dp(k).wait_recv()
+        rate_acc[0] = tree([rate_dp[k] for k in range(m)])
+        copy_rate_x().start()
+        for r in order[: len(order) // 2]:
+            join(1, r)
+        finish(0)
+        copy_rate_x().wait_recv()
+        rate_acc[1] = rate_acc[0] + rate_got[0]
+        for j in range(1, nz):
+            copy_rate_z(j).start()
+        for r in order[len(order) // 2 :]:
+            join(1, r)
+        finish(1)
+        for j in range(1, nz):
+            copy_rate_z(j).wait_recv()
+        drate_ref[...] = tree([rate_acc[1]] + [rate_got[j] for j in range(1, nz)])[:1, :heads]
         for i in range(2):
             for k in range(m):
                 if k:
@@ -474,8 +487,9 @@
         for i in range(2):
             for r in range(1, n):
                 copy_acc(i, r).wait_send()
-        for i in range(stages):
-            copy_rate(i).wait_send()
+        copy_rate_x().wait_send()
+        for j in range(1, nz):
+            copy_rate_z(j).wait_send()
     copy_span().wait_send()
     copy_c().wait_send()
     copy_back(0).wait_send()
@@ -483,11 +497,20 @@
 
     def settle(k, unused):
         copy_g(k).wait_send()
-        pl.when(jnp.logical_not(last))(lambda: copy_e(k).wait_send())
-        pl.when(jnp.logical_not(first))(lambda: copy_f(k).wait_send())
+        for i in range(PARTS):
+            pl.when(jnp.logical_not(last))(lambda: copy_e(k, i).wait_send())
+            pl.when(jnp.logical_not(first))(lambda: copy_f(k, i).wait_send())
         return unused
 
     lax.fori_loop(0, chunks, settle, 0)
+
+
+def store_kernel(*refs):
+    copies = [pltpu.make_async_copy(refs[i], refs[4 + i], refs[8].at[i]) for i in range(4)]
+    for copy in copies:
+        copy.start()
+    for copy in copies:
+        copy.wait()
 
 
 def weight_kernel(
@@ -643,6 +666,7 @@
     rows = pltpu.VMEM((length, full), BF16)
     scratch = (
         [rows, pltpu.VMEM(projection.shape, BF16), rows, rows]
+        + [pltpu.VMEM((heads, length), F32), pltpu.VMEM((1, heads), F32)]
         + [short] * 3
         + [cols] * 2
         + [pltpu.VMEM((groups, HEADS, length), F32), strip, strip, sums, sums]
@@ -651,13 +675,14 @@
         + [by_lane, by_lane, pltpu.VMEM((heads, length), F32), two, two]
         + [rows_in] * 2
         + [slots] * 4
-        + [pltpu.SemaphoreType.DMA((4,)), pltpu.SemaphoreType.DMA((2, 4))]
-        + [pltpu.SemaphoreType.DMA((2, groups))] * 3
+        + [pltpu.SemaphoreType.DMA((6,)), pltpu.SemaphoreType.DMA((2, 4))]
+        + [pltpu.SemaphoreType.DMA((2, groups))]
+        + [pltpu.SemaphoreType.DMA((2, PARTS * groups))] * 2
     )
     rate_shape = jax.ShapeDtypeStruct((8, 2 * heads), F32)
     weight_shape = jax.ShapeDtypeStruct((length, 2 * state), BF16)
     if fused:
-        stages = count.bit_length() - 1
+        pairs = count // 2
         others = members - 1
         scratch += [pltpu.VMEM((others, count, length, piece), F32)] * 2
         scratch += [
@@ -669,19 +694,19 @@
             pltpu.VMEM((2, count - 1, piece, state), F32),
             pltpu.VMEM((2, members, piece, state), F32),
             pltpu.VMEM((members, 8, 2 * heads), F32),
-            pltpu.VMEM((stages, 8, 2 * heads), F32),
-            pltpu.VMEM((stages + 1, 8, 2 * heads), F32),
+            pltpu.VMEM((pairs, 8, 2 * heads), F32),
+            pltpu.VMEM((2, 8, 2 * heads), F32),
             pltpu.SemaphoreType.DMA((2, others)),
             pltpu.SemaphoreType.DMA((2, 2 * others)),
             pltpu.SemaphoreType.DMA((2, 2 * (count - 1))),
             pltpu.SemaphoreType.DMA((2, 2 * members)),
-            pltpu.SemaphoreType.DMA((2, others + stages)),
+            pltpu.SemaphoreType.DMA((2, others + pairs)),
         ]
-        rate_shape = jax.ShapeDtypeStruct((1, heads), F32)
+        rate_shape = pltpu.VMEM((1, heads), F32)
         weight_shape = pltpu.VMEM((members * piece, 2 * state), F32)
     grad_x, grad_logit, rate_rows, weights = pl.pallas_call(
         functools.partial(layer_kernel, count, members, size, fused),
-        in_specs=[away] * 4 + [vmem] * 2,
+        in_specs=[away] * 6,
         out_specs=[vmem] * 4,
         out_shape=[
             rows,
@@ -695,10 +720,21 @@
         ),
         name="layer_gradients",
     )(
-        *(pltpu.with_memory_space_constraint(v, pltpu.HBM) for v in (tokens, projection, x_rows, grad_rows)),
-        logit.T, decay_rate[None, :],
-    )
-    if fused:
+        *(
+            pltpu.with_memory_space_constraint(v, pltpu.HBM)
+            for v in (tokens, projection, x_rows, grad_rows, logit.T, decay_rate[None, :])
+        )
+    )
+    if fused:
+        results = (grad_x, grad_logit, rate_rows, weights)
+        grad_x, grad_logit, rate_rows, weights = pl.pallas_call(
+            store_kernel,
+            in_specs=[vmem] * 4,
+            out_specs=[away] * 4,
+            out_shape=[jax.ShapeDtypeStruct(v.shape, v.dtype) for v in results],
+            scratch_shapes=[pltpu.SemaphoreType.DMA((4,))],
+            name="store_results",
+        )(*results)
         return (grad_x[None], grad_logit.T[None], rate_rows[0], weights)
     chunks = max(1, min(8, piece // 8))
     rows = piece // chunks

time: 106 us -> 101 us (0.953)
  Pallas kernels: 101 us -> 97.4 us
  local copies, waits for them, and re-layouts: 4.3 us -> 2.91 us
    pallas_call x1, Pallas kernels: 101 us -> 94.8 us  [shards(): pl.pallas_call(functools.partial(layer_kernel, count, members, size, fuse...]
    pallas_call x0 -> x1, Pallas kernels: none -> 2.57 us  [shards(): pl.pallas_call(store_kernel, in_specs=[vmem] * 4, out_specs=[away] * 4, o...]
    unnamed x8, local copies, waits for them, and re-layouts: 4.3 us -> 2.91 us
where the time goes in v6:
time: 101 us
  Pallas kernels  97.4 us (96%)
  local copies, waits for them, and re-layouts  2.91 us (3%)
    pallas_call x1, Pallas kernels, shards(): pl.pallas_call(functools.partial(layer_kernel, count, members, size, fuse...  94.8 us
    unnamed x8, local copies, waits for them, and re-layouts  2.91 us
    pallas_call x1, Pallas kernels, shards(): pl.pallas_call(store_kernel, in_specs=[vmem] * 4, out_specs=[away] * 4, o...  2.57 us

profile of v6, /device:TPU:0, one launch (start us, length us, event | category | flops | bytes accessed | tf_op | source)
XLA Modules:
  0.0 100.9 jit_solution(1400942079230515543)
XLA Ops:
  0.6 94.8 %layer_gradients.1 = (bf16[128,4096]{1,0:T(8,128)(2,1)S(1)}, f32[64,128]{1,0:T(8,128)S(1)}, f32[1,64]{1,0:T(1,128)S(1)}, f32[512,256]{1,0:T(8,128)S(1)}) custom-call(bf16[128,4096]{1,0:T(8,128)(2,1)} %bitcast.12, bf16[4096,256]{1,0:T(8,128)(2,1)} %w_hbm.1, bf16[128,4096]{1,0:T(8,128)(2,1)} %bitcast.13, bf16[128,4096]{1,0:T(8,128)(2,1)} %bitcast.14, ...), custom_call_target="tpu_custom_call" | custom-call | tf_op jit(solution)/shard_map/layer_gradients/pallas_call | solution.py:707
  95.4 0.0 copy-start
  95.4 1.0 copy-done
  96.4 0.0 copy-start.1
  96.4 0.8 copy-done.1
  97.2 0.0 copy-start.2
  97.2 0.6 copy-done.2
  97.8 0.0 copy-start.3
  97.8 0.5 copy-done.3
  98.4 2.6 %store_results.1 = (bf16[128,4096]{1,0:T(8,128)(2,1)}, f32[64,128]{1,0:T(8,128)}, f32[1,64]{1,0:T(1,128)}, f32[512,256]{1,0:T(8,128)}) custom-call(bf16[128,4096]{1,0:T(8,128)(2,1)} %copy-done, f32[64,128]{1,0:T(8,128)} %copy-done.2, f32[1,64]{1,0:T(1,128)} %copy-done.3, f32[512,256]{1,0:T(8,128)} %copy-done.1), custom_call_target="tpu_custom_call" | custom-call | tf_op jit(solution)/shard_map/store_results/pallas_call | solution.py:730
Async XLA Ops:
  95.4 1.0 copy-start
  96.4 0.8 copy-start.1
  97.2 0.6 copy-start.2
  97.8 0.5 copy-start.3

commit v7 on v6

--- a/solution.py
+++ b/solution.py
@@ -734,7 +734,7 @@
             out_shape=[jax.ShapeDtypeStruct(v.shape, v.dtype) for v in results],
             scratch_shapes=[pltpu.SemaphoreType.DMA((4,))],
             name="store_results",
-        )(*results)
+        )(*(pltpu.with_memory_space_constraint(v, pltpu.VMEM) for v in results))
         return (grad_x[None], grad_logit.T[None], rate_rows[0], weights)
     chunks = max(1, min(8, piece // 8))
     rows = piece // chunks

time: 101 us -> 96.9 us (0.959)
  local copies, waits for them, and re-layouts: 2.91 us -> 0 us
  Pallas kernels: 97.4 us -> 96 us
    unnamed x8 -> x0, local copies, waits for them, and re-layouts: 2.91 us -> none
    pallas_call x1, Pallas kernels: 2.57 us -> 1.19 us  [shards(): pl.pallas_call(store_kernel, in_specs=[vmem] * 4, out_specs=[away] * 4, o...]
where the time goes in v7:
time: 96.9 us; the launch traced here: 96.6 us
  Pallas kernels  96 us (99%)
    pallas_call x1, Pallas kernels, shards(): pl.pallas_call(functools.partial(layer_kernel, count, members, size, fuse...  94.8 us

profile of v7, /device:TPU:0, one launch (start us, length us, event | category | flops | bytes accessed | tf_op | source)
XLA Modules:
  0.0 96.6 jit_solution(12306943584979434896)
XLA Ops:
  0.6 94.8 %layer_gradients.1 = (bf16[128,4096]{1,0:T(8,128)(2,1)S(1)}, f32[64,128]{1,0:T(8,128)S(1)}, f32[1,64]{1,0:T(1,128)S(1)}, f32[512,256]{1,0:T(8,128)S(1)}) custom-call(bf16[128,4096]{1,0:T(8,128)(2,1)} %bitcast.12, bf16[4096,256]{1,0:T(8,128)(2,1)} %w_hbm.1, bf16[128,4096]{1,0:T(8,128)(2,1)} %bitcast.13, bf16[128,4096]{1,0:T(8,128)(2,1)} %bitcast.14, ...), custom_call_target="tpu_custom_call" | custom-call | tf_op jit(solution)/shard_map/layer_gradients/pallas_call | solution.py:707
  95.4 1.2 %store_results.1 = (bf16[128,4096]{1,0:T(8,128)(2,1)}, f32[64,128]{1,0:T(8,128)}, f32[1,64]{1,0:T(1,128)}, f32[512,256]{1,0:T(8,128)}) custom-call(bf16[128,4096]{1,0:T(8,128)(2,1)S(1)} %get-tuple-element.12.refs_0_, f32[64,128]{1,0:T(8,128)S(1)} %get-tuple-element.13.refs_1_, f32[1,64]{1,0:T(1,128)S(1)} %get-tuple-element.14.refs_2_, ...), custom_call_target="tpu_custom_call" | custom-call | tf_op jit(solution)/shard_map/store_results/pallas_call | solution.py:730

commit v8 on v7

--- a/solution.py
+++ b/solution.py
@@ -11,6 +11,7 @@
 BF16 = jnp.bfloat16
 HEADS = 2
 LAG = 3
+FIRST = 1
 EARLY = 3
 PARTS = 1
 
@@ -51,8 +52,8 @@
 ):
     if fused:
         (
-            tok_snd, tok_in, tok, gbc_snd, gbc_in, gbc, acc, got, out, rate_dp, rate_got, rate_acc,
-            tok_sem, gbc_sem, acc_sem, out_sem, rate_sem,
+            tok_snd, tok_in, tok, gbc_snd, gbc_in, gbc, acc, got, out,
+            tok_sem, gbc_sem, acc_sem, out_sem,
         ) = more
     chunks = gs_snd.shape[0]
     length, state = b_ref.shape
@@ -158,7 +159,7 @@
     pl.when(end)(lambda: pl.semaphore_wait(barrier, min(nz - 1, 1) + greeters))
     pl.when(jnp.logical_not(end))(lambda: pl.semaphore_wait(barrier, 2 + greeters))
     copy_span().start()
-    lax.fori_loop(0, EARLY, scale, 0)
+    lax.fori_loop(0, FIRST, scale, 0)
     load_t.wait()
     load_w.wait()
     bc = dot(t_ref[...], w_ref[...], 1, 0).astype(BF16)
@@ -166,6 +167,7 @@
     c_ref[...] = bc[:, state:]
     cf[...] = bc[:, state:].astype(F32)
     copy_c().start()
+    lax.fori_loop(FIRST, EARLY, scale, 0)
     by_head = q1.T
     for k in range(chunks):
         rows_ref[k] = by_head[HEADS * k : HEADS * (k + 1), :]
@@ -174,8 +176,10 @@
     for ref in (d_scores, d_b, d_c, sums1, sums2, row_sums, back):
         ref[...] = jnp.zeros_like(ref)
     copy_span().wait_recv()
-    copy_c().wait_recv()
-    c_in[...] = cf_in[...].astype(BF16)
+
+    def receive_c():
+        copy_c().wait_recv()
+        c_in[...] = cf_in[...].astype(BF16)
 
     def spans(ref, k):
         return pair_columns(turn(ref[...], k)[:1, :], heads, size)
@@ -302,6 +306,15 @@
 
     delay = LAG * lax.max(z, nz - 1 - z)
 
+    def await_tokens():
+        for k in range(1, m):
+            copy_tokens(k).wait_recv()
+
+    def place_tokens(s):
+        for k in range(m):
+            block = columns(s, k) if k == 0 else tok_in[k - 1, s]
+            tok[s, :, k * length : (k + 1) * length] = block.T.astype(BF16)
+
     def step(t, unused):
         @pl.when(t + EARLY < chunks)
         def _():
@@ -311,9 +324,23 @@
 
         pl.when(jnp.logical_and(kf >= 0, kf < chunks))(lambda: forward(kf))
         kb = t - LAG * (nz - 1 - z)
+        pl.when(kb == 0)(receive_c)
         pl.when(jnp.logical_and(kb >= 0, kb < chunks))(lambda: backward(kb))
         kg = t - delay
         pl.when(jnp.logical_and(kg >= 0, kg < chunks))(lambda: gradients(kg))
+        if fused:
+            @pl.when(t < n)
+            def _():
+                spread(t, 0)
+
+            @pl.when(t == n)
+            def _():
+                for k in range(1, m):
+                    copy_tokens(k).start()
+
+            block = t - (chunks + delay - n)
+            pl.when(block == 0)(await_tokens)
+            pl.when(block >= 0)(lambda: place_tokens(block))
         return unused
 
     if fused:
@@ -337,23 +364,16 @@
 
         def copy_acc(i, r):
             who = partner if r % 2 else flip(me, r, n)
-            return send(acc.at[i, r], got.at[i, r - 1], acc_sem, (n - 1) * i + r - 1, who)
+            rows = pl.ds(0, piece + 8 * i)
+            return send(
+                acc.at[i, r, rows], got.at[i, r - 1, rows], acc_sem, (n - 1) * i + r - 1, who
+            )
 
         def copy_out(i, k):
+            rows = pl.ds(0, piece + 8 * i)
             return send(
-                out.at[i, 0], out.at[i, k], out_sem, m * i + k, flip(dp, k, m), "dp"
+                out.at[i, 0, rows], out.at[i, k, rows], out_sem, m * i + k, flip(dp, k, m), "dp"
             )
-
-        def copy_rate_dp(k):
-            return send(
-                rate_dp.at[0], rate_dp.at[k], rate_sem, k - 1, flip(dp, k, m), "dp"
-            )
-
-        def copy_rate_x():
-            return send(rate_acc.at[0], rate_got.at[0], rate_sem, m - 1, partner)
-
-        def copy_rate_z(j):
-            return send(rate_acc.at[1], rate_got.at[j], rate_sem, m - 1 + j, flip(me, 2 * j, n))
 
         def tree(parts):
             while len(parts) > 1:
@@ -364,10 +384,6 @@
             for k in range(1, m):
                 tok_snd[k - 1, s] = columns(s, k)
             return unused
-
-        lax.fori_loop(0, n, spread, 0)
-        for k in range(1, m):
-            copy_tokens(k).start()
 
     lax.fori_loop(0, chunks + delay, step, 0)
     copy_back(0).start()
@@ -389,28 +405,19 @@
         for k in range(1, m):
             copy_gbc(1, k).start()
         gbc[1, :length] = grad_c
-        for k in range(1, m):
-            copy_tokens(k).wait_recv()
-
-        def place_tokens(r, unused):
-            s = r
-            for k in range(m):
-                block = columns(s, k) if k == 0 else tok_in[k - 1, s]
-                tok[s, :, k * length : (k + 1) * length] = block.T.astype(BF16)
-            return unused
-
-        lax.fori_loop(0, n, place_tokens, 0)
-        order = list(range(n - 2, -1, -2))
-        for i in range(2):
-            for k in range(1, m):
-                copy_gbc(i, k).wait_recv()
-                gbc[i, k * length : (k + 1) * length] = gbc_in[k - 1, i].astype(BF16)
-            for r in [r + 1 for r in order] + order:
-                acc[i, r] = dot(tok[flip(me, r, n)], gbc[i], 1, 0)
-                if r % 2:
-                    copy_acc(i, r).start()
     else:
         weight_ref[:, state:] = grad_c
+    copy_span().wait_send()
+    copy_c().wait_send()
+
+    def settle(k, unused):
+        copy_g(k).wait_send()
+        for i in range(PARTS):
+            pl.when(jnp.logical_not(last))(lambda: copy_e(k, i).wait_send())
+            pl.when(jnp.logical_not(first))(lambda: copy_f(k, i).wait_send())
+        return unused
+
+    lax.fori_loop(0, chunks, settle, 0)
     copy_back(1).wait_recv()
     total = sums2[...] + back_in[1]
     inside, x_in = sums1[:, :heads], sums1[:, heads:]
@@ -428,81 +435,69 @@
     d_rate = jnp.broadcast_to(
         jnp.concatenate([d_rate, jnp.zeros_like(d_rate)], axis=1), (8, 2 * heads)
     )
-    if fused:
-        rate_dp[0] = d_rate
-        for k in range(1, m):
-            copy_rate_dp(k).start()
-    else:
+    if not fused:
         drate_ref[...] = d_rate
     d_step = inside + x_in - rate_ref[...] * d_log
     dlogit_ref[...] = d_step.T * jax.nn.sigmoid(logit_ref[...])
+    copy_back(0).wait_send()
+    copy_back(1).wait_send()
     if fused:
+        for k in range(1, m):
+            copy_tokens(k).wait_send()
+        order = list(range(n - 2, -1, -2))
+        for i in range(2):
+            for k in range(1, m):
+                copy_gbc(i, k).wait_recv()
+                gbc[i, k * length : (k + 1) * length] = gbc_in[k - 1, i].astype(BF16)
+            for r in [r + 1 for r in order] + order:
+                acc[i, r, :piece] = dot(tok[flip(me, r, n)], gbc[i], 1, 0)
+                if i == 1:
+                    acc[i, r, piece:] = d_rate
+                if r % 2:
+                    copy_acc(i, r).start()
 
         def join(i, r):
+            rows = slice(0, piece + 8 * i)
             copy_acc(i, r + 1).wait_recv()
-            acc[i, r] += got[i, r]
+            acc[i, r, rows] += got[i, r, rows]
             if r:
                 copy_acc(i, r).start()
 
         def finish(i):
-            value = acc[i, 0]
-            for r in order[:-1]:
+            rows = slice(0, piece + 8 * i)
+            parts = [acc[i, 0, rows]]
+            for r in range(2, n, 2):
                 copy_acc(i, r).wait_recv()
-                value += got[i, r - 1]
-            out[i, 0] = value
+                parts.append(got[i, r - 1, rows])
+            out[i, 0, rows] = tree(parts)
             for k in range(1, m):
                 copy_out(i, k).start()
 
+        for i in range(2):
+            for k in range(1, m):
+                copy_gbc(i, k).wait_send()
         for r in order:
             join(0, r)
-        for k in range(1, m):
-            copy_rate_dp(k).wait_recv()
-        rate_acc[0] = tree([rate_dp[k] for k in range(m)])
-        copy_rate_x().start()
         for r in order[: len(order) // 2]:
             join(1, r)
         finish(0)
-        copy_rate_x().wait_recv()
-        rate_acc[1] = rate_acc[0] + rate_got[0]
-        for j in range(1, nz):
-            copy_rate_z(j).start()
         for r in order[len(order) // 2 :]:
             join(1, r)
+        for r in range(1, n):
+            copy_acc(0, r).wait_send()
         finish(1)
-        for j in range(1, nz):
-            copy_rate_z(j).wait_recv()
-        drate_ref[...] = tree([rate_acc[1]] + [rate_got[j] for j in range(1, nz)])[:1, :heads]
         for i in range(2):
             for k in range(m):
                 if k:
                     copy_out(i, k).wait_recv()
                 first_row = pl.multiple_of(flip(dp, k, m) * piece, piece)
-                weight_ref[pl.ds(first_row, piece), i * state : (i + 1) * state] = out[i, k]
+                weight_ref[pl.ds(first_row, piece), i * state : (i + 1) * state] = out[i, k, :piece]
+        drate_ref[...] = tree([out[1, k, piece:] for k in range(m)])[:1, :heads]
         for k in range(1, m):
-            copy_tokens(k).wait_send()
-            copy_rate_dp(k).wait_send()
             for i in range(2):
-                copy_gbc(i, k).wait_send()
                 copy_out(i, k).wait_send()
-        for i in range(2):
-            for r in range(1, n):
-                copy_acc(i, r).wait_send()
-        copy_rate_x().wait_send()
-        for j in range(1, nz):
-            copy_rate_z(j).wait_send()
-    copy_span().wait_send()
-    copy_c().wait_send()
-    copy_back(0).wait_send()
-    copy_back(1).wait_send()
-
-    def settle(k, unused):
-        copy_g(k).wait_send()
-        for i in range(PARTS):
-            pl.when(jnp.logical_not(last))(lambda: copy_e(k, i).wait_send())
-            pl.when(jnp.logical_not(first))(lambda: copy_f(k, i).wait_send())
-        return unused
-
-    lax.fori_loop(0, chunks, settle, 0)
+        for r in range(1, n):
+            copy_acc(1, r).wait_send()
 
 
 def store_kernel(*refs):
@@ -662,7 +657,7 @@
     blocks = count * members
     piece = tokens.shape[1] // blocks
     levels = blocks.bit_length() - 1
-    fused = piece % 128 == 0
+    fused = piece % 128 == 0 and 2 * count <= groups
     rows = pltpu.VMEM((length, full), BF16)
     scratch = (
         [rows, pltpu.VMEM(projection.shape, BF16), rows, rows]
@@ -682,7 +677,6 @@
     rate_shape = jax.ShapeDtypeStruct((8, 2 * heads), F32)
     weight_shape = jax.ShapeDtypeStruct((length, 2 * state), BF16)
     if fused:
-        pairs = count // 2
         others = members - 1
         scratch += [pltpu.VMEM((others, count, length, piece), F32)] * 2
         scratch += [
@@ -690,17 +684,13 @@
             pltpu.VMEM((2, length, state), F32),
             pltpu.VMEM((others, 2, length, state), F32),
             pltpu.VMEM((2, members * length, state), BF16),
-            pltpu.VMEM((2, count, piece, state), F32),
-            pltpu.VMEM((2, count - 1, piece, state), F32),
-            pltpu.VMEM((2, members, piece, state), F32),
-            pltpu.VMEM((members, 8, 2 * heads), F32),
-            pltpu.VMEM((pairs, 8, 2 * heads), F32),
-            pltpu.VMEM((2, 8, 2 * heads), F32),
+            pltpu.VMEM((2, count, piece + 8, state), F32),
+            pltpu.VMEM((2, count - 1, piece + 8, state), F32),
+            pltpu.VMEM((2, members, piece + 8, state), F32),
             pltpu.SemaphoreType.DMA((2, others)),
             pltpu.SemaphoreType.DMA((2, 2 * others)),
             pltpu.SemaphoreType.DMA((2, 2 * (count - 1))),
             pltpu.SemaphoreType.DMA((2, 2 * members)),
-            pltpu.SemaphoreType.DMA((2, others + pairs)),
         ]
         rate_shape = pltpu.VMEM((1, heads), F32)
         weight_shape = pltpu.VMEM((members * piece, 2 * state), F32)

time: 96.9 us -> 93.5 us (0.965)
  Pallas kernels: 96 us -> 92.7 us
    pallas_call x1, Pallas kernels: 94.8 us -> 91.5 us  [shards(): pl.pallas_call(functools.partial(layer_kernel, count, members, size, fuse...]
where the time goes in v8:
time: 93.5 us; the launch traced here: 93.3 us
  Pallas kernels  92.7 us (99%)
    pallas_call x1, Pallas kernels, shards(): pl.pallas_call(functools.partial(layer_kernel, count, members, size, fuse...  91.5 us

profile of v8, /device:TPU:0, one launch (start us, length us, event | category | flops | bytes accessed | tf_op | source)
XLA Modules:
  0.0 93.3 jit_solution(15869201035741529592)
XLA Ops:
  0.6 91.5 %layer_gradients.1 = (bf16[128,4096]{1,0:T(8,128)(2,1)S(1)}, f32[64,128]{1,0:T(8,128)S(1)}, f32[1,64]{1,0:T(1,128)S(1)}, f32[512,256]{1,0:T(8,128)S(1)}) custom-call(bf16[128,4096]{1,0:T(8,128)(2,1)} %bitcast.12, bf16[4096,256]{1,0:T(8,128)(2,1)} %w_hbm.1, bf16[128,4096]{1,0:T(8,128)(2,1)} %bitcast.13, bf16[128,4096]{1,0:T(8,128)(2,1)} %bitcast.14, ...), custom_call_target="tpu_custom_call" | custom-call | tf_op jit(solution)/shard_map/layer_gradients/pallas_call | solution.py:697
  92.2 1.2 %store_results.1 = (bf16[128,4096]{1,0:T(8,128)(2,1)}, f32[64,128]{1,0:T(8,128)}, f32[1,64]{1,0:T(1,128)}, f32[512,256]{1,0:T(8,128)}) custom-call(bf16[128,4096]{1,0:T(8,128)(2,1)S(1)} %get-tuple-element.12.refs_0_, f32[64,128]{1,0:T(8,128)S(1)} %get-tuple-element.13.refs_1_, f32[1,64]{1,0:T(1,128)S(1)} %get-tuple-element.14.refs_2_, ...), custom_call_target="tpu_custom_call" | custom-call | tf_op jit(solution)/shard_map/store_results/pallas_call | solution.py:720

commit v9 on v8

--- a/solution.py
+++ b/solution.py
@@ -44,7 +44,7 @@
 def layer_kernel(
     n, m, size, fused, t_hbm, w_hbm, x_hbm, g_hbm, logit_hbm, rate_hbm,
     dx_ref, dlogit_ref, drate_ref, weight_ref, t_ref, w_ref, x_ref, g_ref, logit_ref, rate_ref,
-    b_ref, c_ref, c_in, cols1, cols2, rows_ref, span, span_in, cf, cf_in,
+    b_ref, c_ref, c_in, b_turned, c_turned, c_in_turned, cols1, cols2, rows_ref, span, span_in, cf, cf_in,
     e_own, e_other, f_own, f_other, scores, d_scores, d_b, d_c,
     sums1, sums2, row_sums, back, back_in,
     gs_snd, gs_in, e_in, f_in, e_snd, f_snd,
@@ -168,6 +168,8 @@
     cf[...] = bc[:, state:].astype(F32)
     copy_c().start()
     lax.fori_loop(FIRST, EARLY, scale, 0)
+    b_turned[...] = b_ref[...].astype(F32).T.astype(BF16)
+    c_turned[...] = cf[...].T.astype(BF16)
     by_head = q1.T
     for k in range(chunks):
         rows_ref[k] = by_head[HEADS * k : HEADS * (k + 1), :]
@@ -180,13 +182,14 @@
     def receive_c():
         copy_c().wait_recv()
         c_in[...] = cf_in[...].astype(BF16)
+        c_in_turned[...] = cf_in[...].T.astype(BF16)
 
     def spans(ref, k):
         return pair_columns(turn(ref[...], k)[:1, :], heads, size)
 
     def forward(k):
         weight = pair_columns(cols1[k], heads, size) * pair_columns(cols2[k], 0, size)
-        near = dot(b_ref[...], (x_ref[:, wide(k)].astype(F32) * weight).astype(BF16), 0, 0)
+        near = dot(b_turned[...], (x_ref[:, wide(k)].astype(F32) * weight).astype(BF16), 1, 0)
         mine, theirs = spans(span, k), spans(span_in, k)
 
         @pl.when(first)
@@ -216,8 +219,8 @@
 
     def backward(k):
         copy_g(k).wait_recv()
-        near = dot(c_ref[...], gs_snd[k].astype(BF16), 0, 0)
-        far = dot(c_in[...], gs_in[k].astype(BF16), 0, 0)
+        near = dot(c_turned[...], gs_snd[k].astype(BF16), 1, 0)
+        far = dot(c_in_turned[...], gs_in[k].astype(BF16), 1, 0)
         mine, theirs = spans(span, k), spans(span_in, k)
 
         @pl.when(last)
@@ -392,7 +395,7 @@
     grad_b = (d_b[...] + dot(dk, c_ref[...], 1, 0)).astype(BF16)
     if fused:
         gbc_snd[0] = grad_b.astype(F32)
-        for k in range(1, m):
+        for k in range(m - 1, 0, -1):
             copy_gbc(0, k).start()
         gbc[0, :length] = grad_b
     else:
@@ -402,7 +405,7 @@
     grad_c = (c_total + back_in[0]).astype(BF16)
     if fused:
         gbc_snd[1] = grad_c.astype(F32)
-        for k in range(1, m):
+        for k in range(m - 1, 0, -1):
             copy_gbc(1, k).start()
         gbc[1, :length] = grad_c
     else:
@@ -470,7 +473,7 @@
                 copy_acc(i, r).wait_recv()
                 parts.append(got[i, r - 1, rows])
             out[i, 0, rows] = tree(parts)
-            for k in range(1, m):
+            for k in range(m - 1, 0, -1):
                 copy_out(i, k).start()
 
         for i in range(2):
@@ -663,6 +666,7 @@
         [rows, pltpu.VMEM(projection.shape, BF16), rows, rows]
         + [pltpu.VMEM((heads, length), F32), pltpu.VMEM((1, heads), F32)]
         + [short] * 3
+        + [pltpu.VMEM((state, length), BF16)] * 3
         + [cols] * 2
         + [pltpu.VMEM((groups, HEADS, length), F32), strip, strip, sums, sums]
         + [half] * 4

time: 93.5 us -> 93.3 us (level)
  no operation moved by 1% of the time
where the time goes in v9:
time: 93.3 us; the launch traced here: 93.2 us
  Pallas kernels  92.5 us (99%)
    pallas_call x1, Pallas kernels, shards(): pl.pallas_call(functools.partial(layer_kernel, count, members, size, fuse...  91.4 us

profile of v9, /device:TPU:0, one launch (start us, length us, event | category | flops | bytes accessed | tf_op | source)
XLA Modules:
  0.0 93.2 jit_solution(8682343251282464227)
XLA Ops:
  0.6 91.4 %layer_gradients.1 = (bf16[128,4096]{1,0:T(8,128)(2,1)S(1)}, f32[64,128]{1,0:T(8,128)S(1)}, f32[1,64]{1,0:T(1,128)S(1)}, f32[512,256]{1,0:T(8,128)S(1)}) custom-call(bf16[128,4096]{1,0:T(8,128)(2,1)} %bitcast.12, bf16[4096,256]{1,0:T(8,128)(2,1)} %w_hbm.1, bf16[128,4096]{1,0:T(8,128)(2,1)} %bitcast.13, bf16[128,4096]{1,0:T(8,128)(2,1)} %bitcast.14, ...), custom_call_target="tpu_custom_call" | custom-call | tf_op jit(solution)/shard_map/layer_gradients/pallas_call | solution.py:701
  92.0 1.2 %store_results.1 = (bf16[128,4096]{1,0:T(8,128)(2,1)}, f32[64,128]{1,0:T(8,128)}, f32[1,64]{1,0:T(1,128)}, f32[512,256]{1,0:T(8,128)}) custom-call(bf16[128,4096]{1,0:T(8,128)(2,1)S(1)} %get-tuple-element.12.refs_0_, f32[64,128]{1,0:T(8,128)S(1)} %get-tuple-element.13.refs_1_, f32[1,64]{1,0:T(1,128)S(1)} %get-tuple-element.14.refs_2_, ...), custom_call_target="tpu_custom_call" | custom-call | tf_op jit(solution)/shard_map/store_results/pallas_call | solution.py:724

commit v10 on v9

--- a/solution.py
+++ b/solution.py
@@ -12,7 +12,7 @@
 HEADS = 2
 LAG = 3
 FIRST = 1
-EARLY = 3
+EARLY = 4
 PARTS = 1
 
 

time: 93.3 us -> 93.3 us (level)
  no operation moved by 1% of the time
where the time goes in v10:
time: 93.3 us; the launch traced here: 93.2 us
  Pallas kernels  92.5 us (99%)
    pallas_call x1, Pallas kernels, shards(): pl.pallas_call(functools.partial(layer_kernel, count, members, size, fuse...  91.4 us

profile of v10, /device:TPU:0, one launch (start us, length us, event | category | flops | bytes accessed | tf_op | source)
XLA Modules:
  0.0 93.2 jit_solution(10570463240725801890)
XLA Ops:
  0.6 91.4 %layer_gradients.1 = (bf16[128,4096]{1,0:T(8,128)(2,1)S(1)}, f32[64,128]{1,0:T(8,128)S(1)}, f32[1,64]{1,0:T(1,128)S(1)}, f32[512,256]{1,0:T(8,128)S(1)}) custom-call(bf16[128,4096]{1,0:T(8,128)(2,1)} %bitcast.12, bf16[4096,256]{1,0:T(8,128)(2,1)} %w_hbm.1, bf16[128,4096]{1,0:T(8,128)(2,1)} %bitcast.13, bf16[128,4096]{1,0:T(8,128)(2,1)} %bitcast.14, ...), custom_call_target="tpu_custom_call" | custom-call | tf_op jit(solution)/shard_map/layer_gradients/pallas_call | solution.py:701
  92.0 1.2 %store_results.1 = (bf16[128,4096]{1,0:T(8,128)(2,1)}, f32[64,128]{1,0:T(8,128)}, f32[1,64]{1,0:T(1,128)}, f32[512,256]{1,0:T(8,128)}) custom-call(bf16[128,4096]{1,0:T(8,128)(2,1)S(1)} %get-tuple-element.12.refs_0_, f32[64,128]{1,0:T(8,128)S(1)} %get-tuple-element.13.refs_1_, f32[1,64]{1,0:T(1,128)S(1)} %get-tuple-element.14.refs_2_, ...), custom_call_target="tpu_custom_call" | custom-call | tf_op jit(solution)/shard_map/store_results/pallas_call | solution.py:724
